TPU v7x, 256 devices: a whole 4x4x8 slice. The times are simulated.
256 devices in a mesh: member: 8 (over x, core), lat: 8 (over z_hi, y), lon: 4 (over z_lo).
Axes of the slice: x: 4, y: 4, z: 8 (z_hi: 2, z_lo: 4; z = z_hi * 4 + z_lo), core: 2. Of those that a mesh axis runs over, the one named last changes fastest.
Arguments:
- fields: bfloat16 [8, 240, 480, 384], P('member', 'lat', 'lon'), may hold values from -6 to 6
- targets: float32 [73, 240, 480], P(None, 'lat', 'lon'), may hold values from -6 to 6
- filt_re: float32 [8, 240, 384], P('member', 'lon', 'lat'), may hold values from -6 to 6
- filt_im: float32 [8, 240, 384], P('member', 'lon', 'lat'), may hold values from -6 to 6
- w_in: bfloat16 [8, 384, 384], P('member'), may hold values from -0.3125 to 0.3125
- b_in: float32 [8, 384], P('member'), may hold values from -3 to 3
- w_out: bfloat16 [8, 73, 384], P('member'), may hold values from -0.3125 to 0.3125
- b_out: float32 [8, 73], P('member'), may hold values from -6 to 6
Outputs:
- nll: float32 [73, 240, 480], P(None, 'lat', 'lon')
- grad_re: float32 [8, 240, 384], P('member', 'lon', 'lat')
- grad_im: float32 [8, 240, 384], P('member', 'lon', 'lat')
All inputs are finite; a program needn't handle non-finite values.
Results may differ from a plain program's by a relative error of at most 0.02.
Values may be sent and summed in bfloat16 or wider, within the bound.
A program may use at most 128 MiB of HBM per device.

v0:
```python
import jax
import jax.numpy as jnp
from jax import lax
from jax.sharding import PartitionSpec as P

variance_floor = 0.1


def side_by_side(arrays, axis, split_dim, concat_dim, along):
    ends, at = ([], 0)
    for a in arrays[:-1]:
        at += a.shape[along]
        ends.append(at)
    both = jnp.concatenate(arrays, axis=along)
    return tuple(
        jnp.split(
            lax.all_to_all(both, axis, split_axis=split_dim, concat_axis=concat_dim, tiled=True),
            ends,
            axis=along,
        )
    )


def cut_along(shard, dim, length):
    before, after = (shard.shape[:dim], shard.shape[dim + 1 :])
    return jnp.moveaxis(shard.reshape(*before, length, -1, *after), dim, 0)


def laid_out(blocks, dim):
    lengths = list(blocks.shape[1:])
    lengths[dim] *= blocks.shape[0]
    return jnp.moveaxis(blocks, 0, dim).reshape(lengths)


def joined_exchange(shard, axis, axes, splits, concats):
    sizes = [lax.axis_size(a) for a in axes]
    blocks = cut_along(shard, splits[0], sizes[0])
    blocks = jnp.moveaxis(cut_along(blocks, splits[1] + 1, sizes[1]), 0, 1)
    inside = blocks.shape[2:]
    blocks = blocks.reshape(-1, *inside)
    blocks = lax.all_to_all(blocks, axis, split_axis=0, concat_axis=0, tiled=True)
    blocks = laid_out(blocks.reshape(*sizes, *inside), concats[0] + 1)
    return laid_out(blocks, concats[1])


def filled_up(lines, length):
    spare = -lines.shape[0] % length
    if not spare:
        return lines
    return jnp.concatenate([lines, jnp.zeros((spare, *lines.shape[1:]), lines.dtype)])


def sum_by_parts(shard, axis):
    lines = shard.reshape(-1, *shard.shape[1:][-1:])
    padded = filled_up(lines, lax.axis_size(axis))
    own = lax.psum_scatter(padded, axis, scatter_dimension=0, tiled=True)
    whole = lax.all_gather(own, axis, axis=0, tiled=True)
    return whole[: len(lines)].reshape(shard.shape)


def lat_table(rows):
    degree = jnp.arange(rows, dtype=jnp.float32)[:, None]
    column = jnp.arange(rows, dtype=jnp.float32)[None, :]
    scale = jnp.where(degree == 0, jnp.sqrt(1.0 / rows), jnp.sqrt(2.0 / rows))
    return (scale * jnp.cos(jnp.pi * degree * (column + 0.5) / rows)).astype(jnp.bfloat16)


def lon_table(columns):
    half_modes = columns // 2
    place = jnp.arange(columns, dtype=jnp.int32)[:, None]
    order = jnp.arange(half_modes, dtype=jnp.int32)[None, :]
    angle = 2.0 * jnp.pi * (place * order % columns).astype(jnp.float32) / columns
    scale = jnp.where(order == 0, jnp.sqrt(1.0 / columns), jnp.sqrt(2.0 / columns))
    return jnp.concatenate([scale * jnp.cos(angle), -scale * jnp.sin(angle)], axis=1).astype(
        jnp.bfloat16
    )


def mode_mask(degrees, half_modes):
    degree = jnp.arange(degrees, dtype=jnp.int32)
    order = jnp.arange(2 * half_modes, dtype=jnp.int32) % half_modes
    return (degree[:, None] >= order[None, :]).astype(jnp.float32)


def apply_filter(spectrum, weight_re, weight_im, keep_modes):
    half_modes = spectrum.shape[2] // 2
    spec_re = spectrum[:, :, :half_modes]
    spec_im = spectrum[:, :, half_modes:]
    keep_half = keep_modes[None, :, :half_modes, None]
    wre = weight_re[:, :, None, :]
    wim = weight_im[:, :, None, :]
    out_re = keep_half * (wre * spec_re - wim * spec_im)
    out_im = keep_half * (wre * spec_im + wim * spec_re)
    return jnp.concatenate([out_re, out_im], axis=2).astype(jnp.bfloat16)


def filter_grads(spectrum, g_spec, keep_modes):
    half_modes = spectrum.shape[2] // 2
    keep_half = keep_modes[None, :, :half_modes, None]
    spec_re = spectrum[:, :, :half_modes]
    spec_im = spectrum[:, :, half_modes:]
    grad_sre = g_spec[:, :, :half_modes]
    grad_sim = g_spec[:, :, half_modes:]
    grad_wre = jnp.sum(keep_half * (grad_sre * spec_re + grad_sim * spec_im), axis=2)
    grad_wim = jnp.sum(keep_half * (grad_sim * spec_re - grad_sre * spec_im), axis=2)
    return (grad_wre, grad_wim)


def lat_forward(lat_basis, grid_field):
    return jnp.einsum(
        "kj,mjlc->mklc", lat_basis, grid_field, preferred_element_type=jnp.float32
    ).astype(jnp.bfloat16)


def lon_forward(lon_basis, coef):
    return jnp.einsum("mklc,lq->mkqc", coef, lon_basis, preferred_element_type=jnp.float32)


def lon_inverse(lon_basis, filtered):
    return jnp.einsum(
        "mkqc,lq->mklc", filtered, lon_basis, preferred_element_type=jnp.float32
    ).astype(jnp.bfloat16)


def lat_inverse(lat_basis, lon_back):
    return jnp.einsum(
        "kj,mklc->mjlc", lat_basis, lon_back, preferred_element_type=jnp.float32
    ).astype(jnp.bfloat16)


def on_device(fields, targets, filt_re, filt_im, w_in, b_in, w_out, b_out):
    lat_parts = lax.axis_size("lat")
    lon_parts = lax.axis_size("lon")
    rows = fields.shape[1] * lat_parts
    columns = fields.shape[2] * lon_parts
    width = fields.shape[3]
    half_modes = columns // 2
    lat_basis = lat_table(rows)
    lon_basis = lon_table(columns)
    keep_modes = mode_mask(rows, half_modes)
    weight_re, weight_im = side_by_side((filt_re, filt_im), "lon", 2, 1, 0)

    def to_spectral(grid_field):
        whole_grid = joined_exchange(grid_field, ("lat", "lon"), ("lat", "lon"), (3, 3), (1, 2))
        coef = lat_forward(lat_basis, whole_grid)
        return lon_forward(lon_basis, coef)

    spectrum = to_spectral(fields)
    filtered = apply_filter(spectrum, weight_re, weight_im, keep_modes)
    lon_back = lon_inverse(lon_basis, filtered)
    spatial = lat_inverse(lat_basis, lon_back)
    returned = joined_exchange(spatial, ("lat", "lon"), ("lat", "lon"), (1, 2), (3, 3))
    block = width // (lat_parts * lon_parts)
    shaped = returned.reshape(
        returned.shape[0], returned.shape[1], returned.shape[2], lon_parts, lat_parts, block
    )
    spatial = shaped.transpose(0, 1, 2, 4, 3, 5).reshape(
        returned.shape[0], returned.shape[1], returned.shape[2], width
    )
    mixed = (fields.astype(jnp.float32) + spatial.astype(jnp.float32)).astype(jnp.bfloat16)
    preact = (
        jnp.einsum("mjlc,mcd->mjld", mixed, w_in, preferred_element_type=jnp.float32)
        + b_in[:, None, None, :]
    )
    hidden = jax.nn.silu(preact).astype(jnp.bfloat16)
    predicted = (
        jnp.einsum("mjld,mvd->mvjl", hidden, w_out, preferred_element_type=jnp.float32)
        + b_out[:, :, None, None]
    )
    first_sum, second_sum = (
        sum_by_parts(jnp.sum(predicted, axis=0), "member"),
        sum_by_parts(jnp.sum(predicted * predicted, axis=0), "member"),
    )
    members = fields.shape[0] * lax.axis_size("member")
    variables = targets.shape[0]
    ens_mean = first_sum / members
    variance = second_sum / members - ens_mean * ens_mean + variance_floor
    residual = targets - ens_mean
    inv_var = 1.0 / variance
    nll = 0.5 * (jnp.log(variance) + residual * residual * inv_var)
    g_pred = (
        -residual * inv_var / members
        + (inv_var - residual * residual * inv_var * inv_var) * (predicted - ens_mean) / members
    ) / variables
    g_hidden = jnp.einsum(
        "mvjl,mvd->mjld", g_pred, w_out.astype(jnp.float32), precision=lax.Precision.HIGHEST
    )
    sigma = jax.nn.sigmoid(preact)
    g_preact = (g_hidden * sigma * (1.0 + preact * (1.0 - sigma))).astype(jnp.bfloat16)
    g_mixed = jnp.einsum(
        "mjld,mcd->mjlc", g_preact, w_in, preferred_element_type=jnp.float32
    ).astype(jnp.bfloat16)
    g_spec = to_spectral(g_mixed)
    grad_re, grad_im = filter_grads(spectrum, g_spec, keep_modes)
    grad_re, grad_im = side_by_side((grad_re, grad_im), "lon", 1, 2, 0)
    return (nll, grad_re, grad_im)


def solution(mesh):
    placed = (
        P("member", "lat", "lon", None),
        P(None, "lat", "lon"),
        P("member", "lon", "lat"),
        P("member", "lon", "lat"),
        P("member", None, None),
        P("member", None),
        P("member", None, None),
        P("member", None),
    )
    return jax.shard_map(
        on_device,
        mesh=mesh,
        in_specs=placed,
        out_specs=(P(None, "lat", "lon"), P("member", "lon", "lat"), P("member", "lon", "lat")),
        check_vma=False,
    )
```

profile of v0, /device:TPU:1, one launch (start us, length us, event | category | flops | bytes accessed | tf_op | source)
XLA Modules:
  0.0 501.8 jit_solution(11296740642952690661)
XLA Ops:
  7.2 0.8 pad_maximum_fusion.2
  8.0 0.7 reshape.258
  8.8 6.4 %all-to-all-start = ((f32[4,1,1440]{2,1,0:T(1,128)}), f32[4,1,1440]{2,1,0:T(1,128)S(1)}, u32[]{:S(2)}, u32[]{:S(2)}) async-start(f32[4,1,1440]{2,1,0:T(1,128)} %reshape.258), calls=%async_computation | async-start | bytes 49152 | tf_op jit(solution)/shard_map/all_to_all | solution.py:17
  15.2 3.7 copy.211
  18.9 0.9 fusion.97
  19.8 1.2 pad_maximum_fusion
  21.0 2.8 copy.212
  23.8 3.6 copy.213
  27.4 20.6 %all-to-all-start.1 = ((bf16[32,1,30,120,12]{3,2,4,1,0:T(8,128)(2,1)}), bf16[32,1,30,120,12]{3,2,4,1,0:T(8,128)(2,1)S(1)}, u32[]{:S(2)}, u32[]{:S(2)}) async-start(bf16[32,1,30,120,12]{3,2,4,1,0:T(8,128)(2,1)} %copy.213), calls=%async_computation.1 | async-start | bytes 6291456 | tf_op jit(solution)/shard_map/all_to_all | solution.py:41
  48.0 0.8 fusion.54
  48.8 2.8 multiply_convert_fusion.8
  52.1 0.7 reduce.3
  53.2 67.9 %all-to-all-done.1 = bf16[32,1,30,120,12]{3,2,4,1,0:T(8,128)(2,1)S(1)} async-done(((bf16[32,1,30,120,12]{3,2,4,1,0:T(8,128)(2,1)}), bf16[32,1,30,120,12]{3,2,4,1,0:T(8,128)(2,1)S(1)}, u32[]{:S(2)}, u32[]{:S(2)}) %all-to-all-start.1) | async-done | bytes 2764832 | tf_op jit(solution)/shard_map/all_to_all | solution.py:41
  121.1 1.9 copy.214
  123.0 1.0 copy.215
  124.1 3.9 copy.216
  128.0 8.1 %fusion.20 = f32[1,240,480,12]{1,2,3,0:T(8,128)} fusion(bf16[240,480,12]{0,1,2:T(8,128)(2,1)} %bitcast.167, bf16[480,240]{0,1:T(8,128)(2,1)S(1)} %copy-done.6, bf16[480,240]{0,1:T(8,128)(2,1)} %get-tuple-element.49, f32[240]{0:T(256)S(1)} %get-tuple-element.51, f32[240]{0:T(256)S(1)} %iota_multiply_fusion, f32[240]{0:T(256)S(1)} %get-tuple-element.50), kind=kOutput, calls=%fused_computation.29 | convolution fusion | flops 1993190400 | bytes 8758080 | tf_op jit(solution)/shard_map/mklc,lq->mkqc/dot_general | solution.py:116
  136.1 3.7 fusion.39
  139.8 6.0 %convert_bitcast_fusion = bf16[1,240,480,12]{1,2,3,0:T(8,128)(2,1)} fusion(bf16[240,240,12]{0,1,2:T(8,128)(2,1)S(1)} %get-tuple-element.33, bf16[240,240,12]{0,1,2:T(8,128)(2,1)S(1)} %get-tuple-element.32, bf16[480,240]{0,1:T(8,128)(2,1)} %get-tuple-element.48, bf16[480,240]{0,1:T(8,128)(2,1)} %get-tuple-element.49, f32[240]{0:T(256)S(1)} %get-tuple-element.51, ...), kind=kOutput, calls=%fused_computation.20 | convolution fusion | flops 2000102400 | bytes 5993280 | tf_op jit(solution)/shard_map/kj,mklc->mjlc/dot_general | solution.py:126
  145.8 3.1 copy.221
  148.9 3.6 reshape_transpose_reshape.3
  152.5 3.4 copy.222
  155.9 3.6 copy.223
  159.5 5.0 all-to-all-start.2
  164.8 71.4 %all-to-all-done.2 = bf16[32,1,30,120,12]{3,2,4,1,0:T(8,128)(2,1)S(1)} async-done(((bf16[32,1,30,120,12]{3,2,4,1,0:T(8,128)(2,1)}), bf16[32,1,30,120,12]{3,2,4,1,0:T(8,128)(2,1)S(1)}, u32[]{:S(2)}, u32[]{:S(2)}) %all-to-all-start.2) | async-done | bytes 2764832 | tf_op jit(solution)/shard_map/all_to_all | solution.py:41
  236.3 2.3 copy.256
  238.5 7.2 %copy.225 = f32[1,30,120,8,4,12]{2,0,5,4,3,1:T(1,128)} copy(f32[1,30,120,8,4,12]{2,4,5,3,1,0:T(4,128)S(1)} %bitcast.154) | data formatting | bytes 11059200 | tf_op jit(solution)/shard_map/convert_element_type | solution.py:160
  245.8 13.0 %copy.226 = f32[1,30,120,384]{3,2,1,0:T(8,128)} copy(f32[1,30,120,384]{2,0,3,1:T(1,128)} %bitcast.153) | data formatting | bytes 11059200 | tf_op jit(solution)/shard_map/convert_element_type | solution.py:160
  258.8 4.7 fusion.16
  263.5 1.8 fusion.18
  266.3 1.1 reshape.234
  267.3 1.2 reshape.235
  268.5 1.4 concatenate.39
  270.1 1.1 concatenate.40
  271.1 21.4 %fusion.93 = (f32[288,120]{1,0:T(8,128)S(1)}, f32[288,120]{1,0:T(8,128)S(1)}) fusion(f32[2192,120]{1,0:T(8,128)S(1)} %concatenate.39, f32[2192,120]{1,0:T(8,128)} %concatenate.40), kind=kCustom, calls=%all-reduce-scatter.2 | all-reduce-scatter fusion | flops 552961 | bytes 2381824
  292.6 3.3 collective-permute-start.1
  297.6 0.7 dynamic-slice_bitcast_fusion
  298.4 4.6 collective-permute-start
  303.0 0.8 collective-permute-done
  304.2 0.7 dynamic-slice_bitcast_fusion.1
  304.9 18.4 %all-gather.7.cloned.1.call-done = f32[8,274,120]{2,1,0:T(8,128)} async-done(((f32[1,274,120]{2,1,0:T(8,128)}), f32[8,274,120]{2,1,0:T(8,128)}) %all-gather.7.cloned.1.call-update) | async-done | bytes 1052176 | tf_op jit(solution)/shard_map/all_gather | solution.py:57
  323.2 1.3 reshape.249
  324.6 1.1 slice_multiply_fusion
  325.6 25.5 %all-gather.5.cloned.1.call-done = f32[8,274,120]{2,1,0:T(8,128)} async-done(((f32[1,274,120]{2,1,0:T(8,128)}), f32[8,274,120]{2,1,0:T(8,128)}) %all-gather.5.cloned.1.call-update) | async-done | bytes 1052176 | tf_op jit(solution)/shard_map/all_gather | solution.py:57
  351.1 1.3 reshape.247
  352.5 1.1 slice_multiply_fusion.1
  353.5 1.4 div.57
  354.9 2.3 div.59
  357.2 3.4 fusion.45
  360.6 2.9 fusion.41
  363.5 7.2 %fusion.38 = bf16[30,120,384]{2,1,0:T(8,128)(2,1)} fusion(f32[30,120,384]{2,1,0:T(8,128)S(1)} %fusion.41, f32[30,120,384]{2,1,0:T(8,128)} %copy-done.2, f32[384]{0:T(512)S(1)} %reduce.2, bf16[1,384,384]{2,1,0:T(8,128)(2,1)S(1)} %copy-done), kind=kOutput, calls=%fused_computation.33 | convolution fusion | flops 1076889600 | bytes 14120448 | tf_op jit(solution)/shard_map/mjld,mcd->mjlc/dot_general | solution.py:190
  370.7 3.7 copy.229
  374.5 0.9 fusion.96
  375.4 1.3 pad_maximum_fusion.1
  376.7 2.8 copy.230
  379.5 1.9 copy.231
  381.5 82.7 %all_to_all.45 = bf16[32,1,30,120,12]{3,2,4,1,0:T(8,128)(2,1)S(1)} all-to-all(bf16[32,1,30,120,12]{3,2,4,1,0:T(8,128)(2,1)S(1)} %copy.231), channel_id=1, replica_groups=mesh['member'=8,'lat'=8,'lon'=4] {'lat','lon'}, dimensions={0} | all-to-all | bytes 5529600 | tf_op jit(solution)/shard_map/all_to_all | solution.py:41
  464.2 1.9 copy.232
  466.1 1.0 copy.233
  467.1 3.9 copy.234
  471.0 8.1 %fusion.23 = f32[1,240,480,12]{1,2,3,0:T(8,128)} fusion(bf16[240,480,12]{0,1,2:T(8,128)(2,1)} %bitcast.166, bf16[480,240]{0,1:T(8,128)(2,1)S(1)} %copy-done.7, bf16[480,240]{0,1:T(8,128)(2,1)} %get-tuple-element.49, f32[240]{0:T(256)S(1)} %get-tuple-element.51, f32[240]{0:T(256)S(1)} %iota_multiply_fusion, f32[240]{0:T(256)S(1)} %get-tuple-element.50), kind=kOutput, calls=%fused_computation.30 | convolution fusion | flops 1993190400 | bytes 8758080 | tf_op jit(solution)/shard_map/mklc,lq->mkqc/dot_general | solution.py:116
  479.1 5.8 %multiply_reduce_fusion.1 = (f32[240,12]{0,1:T(8,128)S(1)}, f32[240,12]{0,1:T(8,128)S(1)}) fusion(f32[1,240,480,12]{1,2,3,0:T(8,128)} %fusion.23, f32[1,240,480,12]{1,2,3,0:T(8,128)} %fusion.20, f32[240,240]{0,1:T(8,128)S(1)} %copy-done.5), kind=kLoop, calls=%fused_computation.18 | loop fusion | flops 6906240 | bytes 11312640 | tf_op jit(solution)/shard_map/reduce_sum | solution.py:104
  485.4 6.8 %all_to_all.46 = f32[4,1,1440]{2,1,0:T(1,128)S(1)} all-to-all(f32[4,1,1440]{2,1,0:T(1,128)S(1)} %reshape.260), channel_id=1, replica_groups=mesh['member'=8,'lat'=8,'lon'=4] {'lon'}, dimensions={0} | all-to-all | bytes 46080 | tf_op jit(solution)/shard_map/all_to_all | solution.py:17
  492.2 0.7 reduce.4
  (59 shorter events, 6.2 us)
Async XLA Ops:
  7.2 251.6 %copy-start = (bf16[1,384,384]{2,1,0:T(8,128)(2,1)S(1)}, bf16[1,384,384]{2,1,0:T(8,128)(2,1)}, u32[]{:S(2)}) copy-start(bf16[1,384,384]{2,1,0:T(8,128)(2,1)} %param.12) | copy-start | bytes 884740
  8.8 18.6 %all-to-all-start = ((f32[4,1,1440]{2,1,0:T(1,128)}), f32[4,1,1440]{2,1,0:T(1,128)S(1)}, u32[]{:S(2)}, u32[]{:S(2)}) async-start(f32[4,1,1440]{2,1,0:T(1,128)} %reshape.258), calls=%async_computation | async-start | bytes 49152 | tf_op jit(solution)/shard_map/all_to_all | solution.py:17
  27.4 93.8 %all-to-all-start.1 = ((bf16[32,1,30,120,12]{3,2,4,1,0:T(8,128)(2,1)}), bf16[32,1,30,120,12]{3,2,4,1,0:T(8,128)(2,1)S(1)}, u32[]{:S(2)}, u32[]{:S(2)}) async-start(bf16[32,1,30,120,12]{3,2,4,1,0:T(8,128)(2,1)} %copy.213), calls=%async_computation.1 | async-start | bytes 6291456 | tf_op jit(solution)/shard_map/all_to_all | solution.py:41
  124.1 3.9 copy-start.6
  128.0 8.1 %copy-start.4 = (f32[240,240]{0,1:T(8,128)S(1)}, f32[240,240]{0,1:T(8,128)}, u32[]{:S(2)}) copy-start(f32[240,240]{0,1:T(8,128)} %fusion.54) | copy-start | bytes 691204
  159.5 5.2 %copy-start.9 = (f32[1,384]{1,0:T(1,128)S(1)}, f32[1,384]{1,0:T(1,128)}, u32[]{:S(2)}) copy-start(f32[1,384]{1,0:T(1,128)} %param.13) | copy-start | bytes 4612
  159.5 76.7 %all-to-all-start.2 = ((bf16[32,1,30,120,12]{3,2,4,1,0:T(8,128)(2,1)}), bf16[32,1,30,120,12]{3,2,4,1,0:T(8,128)(2,1)S(1)}, u32[]{:S(2)}, u32[]{:S(2)}) async-start(bf16[32,1,30,120,12]{3,2,4,1,0:T(8,128)(2,1)} %copy.223), calls=%async_computation.2 | async-start | bytes 6291456 | tf_op jit(solution)/shard_map/all_to_all | solution.py:41
  164.5 158.7 %all-gather.7.cloned.1.call-start = ((), (), s32[]{:S(2)}) async-start(), calls=%async_computation.6 | async-start | bytes 1290240 | tf_op jit(solution)/shard_map/all_gather | solution.py:57
  245.8 13.0 %copy-start.1 = (bf16[1,30,120,384]{3,2,1,0:T(8,128)(2,1)S(1)}, bf16[1,30,120,384]{3,2,1,0:T(8,128)(2,1)}, u32[]{:S(2)}) copy-start(bf16[1,30,120,384]{3,2,1,0:T(8,128)(2,1)} %param.8) | copy-start | bytes 8294404
  258.8 4.7 copy-start.8
  263.5 2.4 copy-start.2
  263.5 2.4 copy-start.10
  268.5 1.6 copy-start.3
  270.1 25.8 %copy-start.11 = (u32[256]{0:T(256)S(1)}, u32[256]{0:T(256)}, u32[]{:S(2)}) copy-start(u32[256]{0:T(256)} %constant.79) | copy-start | bytes 3076
  292.6 4.6 collective-permute-start.1
  298.3 52.8 %all-gather.5.cloned.1.call-start = ((), (), s32[]{:S(2)}) async-start(), calls=%async_computation.5 | async-start | bytes 1290240 | tf_op jit(solution)/shard_map/all_gather | solution.py:57
  298.4 5.4 %collective-permute-start = (f32[98,120]{1,0:T(8,128)S(1)}, f32[98,120]{1,0:T(8,128)S(1)}, u32[]{:S(2)}, u32[]{:S(2)}) collective-permute-start(f32[98,120]{1,0:T(8,128)S(1)} %slice.98), channel_id=1, source_target_pairs={{0,32},{32,64},{64,96},{96,128},{128,160},{160,192},{192,224},{1,3... | collective-permute-start | bytes 141128
  467.1 3.9 copy-start.7
  471.0 8.1 %copy-start.5 = (f32[240,240]{0,1:T(8,128)S(1)}, f32[240,240]{0,1:T(8,128)}, u32[]{:S(2)}) copy-start(f32[240,240]{0,1:T(8,128)} %fusion.54) | copy-start | bytes 691204
Sparse Core Ops, SparseCore 0:
  298.4 24.7 all-gather.6
  325.1 26.0 all-gather.4
where the time goes:
time: 504 us; the launch traced here: 502 us
  waiting for transfers between devices  184 us (37%)
  blocking collectives  111 us (22%)
  local copies, waits for them, and re-layouts  88.8 us (18%)
  starting transfers between devices  40.2 us (8%)
  matrix products  38.7 us (8%)
  other arithmetic  23.8 us (5%)
  between operations  15.3 us (3%)
    all_to_all x2, waiting for transfers between devices, joined_exchange(): lax.all_to_all(blocks, axis, split_axis=0, concat_axis=0, tiled=True)  139 us
    all_to_all x1, blocking collectives, joined_exchange(): lax.all_to_all(blocks, axis, split_axis=0, concat_axis=0, tiled=True)  82.7 us
    all_gather x2, waiting for transfers between devices, sum_by_parts(): whole = lax.all_gather(own, axis, axis=0, tiled=True)  43.9 us
    all_to_all x2, starting transfers between devices, joined_exchange(): lax.all_to_all(blocks, axis, split_axis=0, concat_axis=0, tiled=True)  25.6 us
    convert_element_type x3, local copies, waits for them, and re-layouts, on_device(): spatial.astype(jnp.float32)  22.5 us
    unnamed x1, blocking collectives  21.4 us
    dot_general x2, matrix products, lon_forward(): jnp.einsum('mklc,lq->mkqc', coef, lon_basis, preferred_element_type=jnp.f...  16.1 us
    unnamed x38, local copies, waits for them, and re-layouts  11.5 us
  transfers between devices with their start and end apart: 7, of which 5 were waited for; matrix products, arithmetic and copies ran while one was open for 4% of the time, Pallas kernels for 0%

commit v1 on v0

v1 whole, which is shorter than its diff:
```python
import functools

import jax
import jax.numpy as jnp
import numpy as np
from jax import lax
from jax.experimental import pallas as pl
from jax.experimental.pallas import tpu as pltpu
from jax.sharding import PartitionSpec as P

MESH_ID = pl.DeviceIdType.MESH
F32 = jnp.float32
BF16 = jnp.bfloat16

rows, columns, width, variables, members = 240, 480, 384, 73, 8
own_rows, own_columns, own_width = 30, 120, 12
chunks = 3
chunk = own_width // chunks
variance_floor = 0.1


def tables():
    k = np.arange(rows, dtype=np.float64)[:, None]
    j = np.arange(rows, dtype=np.float64)[None, :]
    lat = np.where(k == 0, np.sqrt(1.0 / rows), np.sqrt(2.0 / rows)) * np.cos(
        np.pi * k * (j + 0.5) / rows
    )
    half = columns // 2
    place = np.arange(columns, dtype=np.int64)[:, None]
    order = np.arange(half, dtype=np.int64)[None, :]
    angle = 2.0 * np.pi * (place * order % columns).astype(np.float64) / columns
    scale = np.where(order == 0, np.sqrt(1.0 / columns), np.sqrt(2.0 / columns))
    kpad = (np.arange(rows) // 60) * 64 + np.arange(rows) % 60
    jpad = (np.arange(rows) // 30) * 32 + np.arange(rows) % 30
    lpad = (np.arange(columns) // 120) * 128 + np.arange(columns) % 120
    lat_pad = np.zeros((256, 256), np.float32)
    lat_pad[np.ix_(kpad, jpad)] = lat
    lon_pad = np.zeros((512, 512), np.float32)
    lon_pad[np.ix_(lpad, np.arange(half))] = scale * np.cos(angle)
    lon_pad[np.ix_(lpad, 256 + np.arange(half))] = -scale * np.sin(angle)
    return lat_pad, lon_pad


def mm(a, b):
    return jnp.dot(a, b, preferred_element_type=F32)


def wait_for(ref, sem):
    pltpu.make_async_copy(ref, ref, sem).wait()


def kernel(
    fields, targets, filters, w, w_t, b, wo, wo_t, bo, lat, lat_t, lon, lon_t,
    nll, grads,
    cells, fields_t, block, grid, spatial, back, spectrum, preact, pred, pred_in, sums, ggrid,
    weights, gsum, gsum_in, mixed, gpair,
    out_sem, in_sem, back_out, back_in, gout_sem, gin_sem, pred_out, pred_in_sem,
    sums_out, sums_in, fwd_out, fwd_in, filt_out, filt_in, grad_out, grad_in,
):
    im = lax.axis_index("member")
    ilat = lax.axis_index("lat")
    ilon = lax.axis_index("lon")
    me = ilat * 4 + ilon
    partner = (im // 2) * 2 + 1 - im % 2

    def peer(o):
        y, z = ilat % 4, (ilat // 4) * 4 + ilon
        y2, z2 = (y + o % 4) % 4, (z + o // 4) % 8
        la, lo = (z2 // 4) * 4 + y2, z2 % 4
        return (im, la, lo), la, lo

    def at_member(m):
        return (m, ilat, ilon)

    barrier = pltpu.get_barrier_semaphore()

    @pl.loop(1, 32)
    def _(o):
        pl.semaphore_signal(barrier, 1, device_id=peer(o)[0], device_id_type=MESH_ID)

    @pl.loop(1, 8)
    def _(o):
        pl.semaphore_signal(
            barrier, 1, device_id=at_member((im + o) % 8), device_id_type=MESH_ID
        )

    def grid_part(ref, ch, la, lo):
        return ref.at[
            pl.ds(ch * chunk, chunk),
            pl.ds(pl.multiple_of(la * 32, 32), 32),
            pl.ds(pl.multiple_of(lo * 128, 128), 128),
        ]

    def block_part(ref, ch, la, lo):
        return ref.at[pl.ds((la * 4 + lo) * own_width + ch * chunk, chunk)]

    @pl.loop(0, own_rows)
    def _(j):
        x = fields[j].astype(F32)
        x = jnp.concatenate([x, jnp.zeros((8, width), F32)], axis=0).T
        cells[pl.ds(j, width, stride=32), :] = x
        fields_t[j // 4, :, pl.ds(pl.multiple_of((j % 4) * 128, 128), 128)] = x.astype(BF16)

    for j in (30, 31):
        cells[pl.ds(j, width, stride=32), :] = jnp.zeros((width, 128), F32)
    fields_t[7, :, 256:512] = jnp.zeros((width, 256), BF16)

    def fill_block():
        @pl.loop(0, width // 8)
        def _(i):
            part = cells[pl.ds(pl.multiple_of(i * 256, 256), 256), :]
            block[pl.ds(i * 8, 8)] = part.astype(BF16).reshape(8, 32, 128)

    fill_block()
    pl.semaphore_wait(barrier, 31 + 7)

    def filter_copy(o):
        lo = (ilon + o) % 4
        return pltpu.make_async_remote_copy(
            filters,
            weights.at[:, pl.ds(pl.multiple_of(ilon * 64, 64), 64), :],
            filt_out,
            filt_in,
            device_id=(im, ilat, lo),
            device_id_type=MESH_ID,
        )

    @pl.loop(1, 4)
    def _(o):
        filter_copy(o).start()

    weights[:, pl.ds(pl.multiple_of(ilon * 64, 64), 64), :] = filters[...]

    def send_blocks(target, sems_out, sems_in):
        for ch in range(chunks):

            @pl.loop(1, 32)
            def _(o):
                dev, la, lo = peer(o)
                pltpu.make_async_remote_copy(
                    block_part(block, ch, la, lo),
                    grid_part(target, ch, ilat, ilon),
                    sems_out.at[ch],
                    sems_in.at[ch],
                    device_id=dev,
                    device_id_type=MESH_ID,
                ).start()

            target[
                pl.ds(ch * chunk, chunk),
                pl.ds(pl.multiple_of(ilat * 32, 32), 32),
                pl.ds(pl.multiple_of(ilon * 128, 128), 128),
            ] = block[pl.ds(me * own_width + ch * chunk, chunk)]

    def of_31(ref):
        return ref.at[pl.ds(0, 31 * chunk)]

    send_blocks(grid, out_sem, in_sem)
    wait_for(weights.at[:, pl.ds(0, 192), :], filt_in)

    lane = lax.broadcasted_iota(jnp.int32, (256, 128), 1)
    k_row = lax.broadcasted_iota(jnp.int32, (256, 256), 0)
    keep = (k_row // 64) * 60 + k_row % 64 >= lax.broadcasted_iota(jnp.int32, (256, 256), 1)

    def to_spectral(x):
        return mm(mm(lat[...], x).astype(BF16), lon[...])

    for ch in range(chunks):
        wait_for(of_31(block), in_sem.at[ch])

        @pl.loop(ch * chunk, (ch + 1) * chunk)
        def _(c):
            own = lane == ilon * own_width + c
            wr = jnp.sum(jnp.where(own, weights[0], 0.0), axis=1, keepdims=True)
            wi = jnp.sum(jnp.where(own, weights[1], 0.0), axis=1, keepdims=True)
            spectrum[c] = to_spectral(grid[c])
            sr, si = spectrum[c, :, 0:256], spectrum[c, :, 256:512]
            fr = jnp.where(keep, wr * sr - wi * si, 0.0).astype(BF16)
            fi = jnp.where(keep, wr * si + wi * sr, 0.0).astype(BF16)
            lon_back = mm(jnp.concatenate([fr, fi], axis=1), lon_t[...]).astype(BF16)
            spatial[c] = mm(lat_t[...], lon_back).astype(BF16)

        @pl.loop(1, 32)
        def _(o):
            dev, la, lo = peer(o)
            pltpu.make_async_remote_copy(
                grid_part(spatial, ch, la, lo),
                block_part(back, ch, ilat, ilon),
                back_out.at[ch],
                back_in.at[ch],
                device_id=dev,
                device_id_type=MESH_ID,
            ).start()

        back[pl.ds(me * own_width + ch * chunk, chunk)] = spatial[
            pl.ds(ch * chunk, chunk),
            pl.ds(pl.multiple_of(ilat * 32, 32), 32),
            pl.ds(pl.multiple_of(ilon * 128, 128), 128),
        ]

    for ch in range(chunks):
        wait_for(of_31(back), back_in.at[ch])

        @pl.loop(0, 32)
        def _(s):
            first = s * own_width + ch * chunk
            cells[pl.ds(pl.multiple_of(first * 32, 128), 128), :] = (
                back[pl.ds(first, chunk)].reshape(chunk * 32, 128).astype(F32)
            )

    def decode(r):
        for q in range(4):
            part = fields_t[r, :, q * 128 : (q + 1) * 128].astype(F32)
            part = part + cells[pl.ds(4 * r + q, width, stride=32), :]
            mixed[:, q * 128 : (q + 1) * 128] = part.astype(BF16)
        pa = mm(w_t[...], mixed[...]) + b[...]
        preact[r] = pa
        hidden = (pa / (1.0 + jnp.exp(-pa))).astype(BF16)
        pred[r] = mm(wo[...], hidden) + bo[...]

    @pl.loop(1, 9)
    def _(o):
        r = (im + o) % 8
        decode(r)

        @pl.when(o < 8)
        def _():
            pltpu.make_async_remote_copy(
                pred.at[r],
                pred_in.at[im],
                pred_out,
                pred_in_sem,
                device_id=at_member(r),
                device_id_type=MESH_ID,
            ).start()

    pred_in[im] = pred[im]
    wait_for(pred.at[pl.ds(0, 7)], pred_in_sem)
    first = pred_in[0]
    second = first * first
    for s in range(1, members):
        first = first + pred_in[s]
        second = second + pred_in[s] * pred_in[s]
    sums[im, 0] = first
    sums[im, 1] = second

    def sums_copy(index, m, sem_out, sem_in):
        return pltpu.make_async_remote_copy(
            sums.at[index],
            sums.at[index],
            sem_out,
            sem_in,
            device_id=at_member(m),
            device_id_type=MESH_ID,
        )

    for t in (1, 2, 3):
        sums_copy(im, (im + 2 * t) % 8, sums_out.at[t], sums_in.at[t]).start()
    sums_copy(im, partner, sums_out.at[0], sums_in.at[0]).start()

    def backward(r):
        mean = sums[r, 0] / members
        var = sums[r, 1] / members - mean * mean + variance_floor
        goal = jnp.concatenate(
            [targets[pl.ds(4 * r + q, 80, stride=32), :] for q in range(4)], axis=1
        )
        res = goal - mean
        inv = 1.0 / var
        loss = 0.5 * (jnp.log(var) + res * res * inv)
        for q in range(4):
            nll[pl.ds(4 * r + q, 80, stride=32), :] = loss[:, q * 128 : (q + 1) * 128]
        gp = (
            -res * inv / members
            + (inv - res * res * inv * inv) * (pred[r] - mean) / members
        ) / variables
        high = gp.astype(BF16)
        gpair[0:80, :] = high
        gpair[80:160, :] = (gp - high.astype(F32)).astype(BF16)
        gh = mm(wo_t[...], gpair[...])
        pa = preact[r]
        sg = 1.0 / (1.0 + jnp.exp(-pa))
        gpre = (gh * sg * (1.0 + pa * (1.0 - sg))).astype(BF16)
        gm = mm(w[...], gpre)
        for q in range(4):
            cells[pl.ds(4 * r + q, width, stride=32), :] = gm[:, q * 128 : (q + 1) * 128]

    @pl.loop(0, 8)
    def _(u):
        t = u // 2
        straight = (im + 8 - 2 * t) % 8
        passed = (partner + 8 - 2 * t) % 8
        even = u % 2 == 0

        @pl.when(jnp.logical_and(even, u > 0))
        def _():
            wait_for(sums.at[0], sums_in.at[t])
            sums_copy(straight, partner, fwd_out.at[t], fwd_in.at[t]).start()

        @pl.when(u == 1)
        def _():
            wait_for(sums.at[0], sums_in.at[0])

        @pl.when(jnp.logical_and(u % 2 == 1, u > 1))
        def _():
            wait_for(sums.at[0], fwd_in.at[t])

        backward(jnp.where(even, straight, passed))

    for ch in range(chunks):
        wait_for(of_31(block), out_sem.at[ch])
    fill_block()
    send_blocks(ggrid, gout_sem, gin_sem)

    gsum[...] = jnp.zeros_like(gsum)
    for ch in range(chunks):
        wait_for(of_31(block), gin_sem.at[ch])

        @pl.loop(ch * chunk, (ch + 1) * chunk)
        def _(c):
            own = lane == ilon * own_width + c
            g = to_spectral(ggrid[c])
            gr, gi = g[:, 0:256], g[:, 256:512]
            sr, si = spectrum[c, :, 0:256], spectrum[c, :, 256:512]
            g_re = jnp.sum(jnp.where(keep, gr * sr + gi * si, 0.0), axis=1, keepdims=True)
            g_im = jnp.sum(jnp.where(keep, gi * sr - gr * si, 0.0), axis=1, keepdims=True)
            gsum[0] = gsum[0] + jnp.where(own, g_re, 0.0)
            gsum[1] = gsum[1] + jnp.where(own, g_im, 0.0)

    @pl.loop(1, 4)
    def _(o):
        lo = (ilon + o) % 4
        pltpu.make_async_remote_copy(
            gsum.at[:, pl.ds(pl.multiple_of(lo * 64, 64), 64), :],
            gsum_in.at[ilon],
            grad_out,
            grad_in,
            device_id=(im, ilat, lo),
            device_id_type=MESH_ID,
        ).start()

    gsum_in[ilon] = gsum[:, pl.ds(pl.multiple_of(ilon * 64, 64), 64), :]
    wait_for(gsum_in.at[pl.ds(0, 3)], grad_in)
    grads[...] = gsum_in[0] + gsum_in[1] + gsum_in[2] + gsum_in[3]

    for ch in range(chunks):
        wait_for(of_31(back), back_out.at[ch])
        wait_for(of_31(block), gout_sem.at[ch])
    wait_for(pred.at[pl.ds(0, 7)], pred_out)
    for t in range(4):
        wait_for(sums.at[0], sums_out.at[t])
    for t in (1, 2, 3):
        wait_for(sums.at[0], fwd_out.at[t])
    wait_for(weights.at[:, pl.ds(0, 192), :], filt_out)
    wait_for(gsum_in.at[pl.ds(0, 3)], grad_out)


def on_device(fields, targets, filt_re, filt_im, w_in, b_in, w_out, b_out):
    lat_pad, lon_pad = tables()
    lat = jnp.asarray(lat_pad, BF16)
    lat_t = jnp.asarray(lat_pad.T.copy(), BF16)
    lon = jnp.asarray(lon_pad, BF16)
    lon_t = jnp.asarray(lon_pad.T.copy(), BF16)
    filters = jnp.pad(jnp.concatenate([filt_re, filt_im], axis=0), ((0, 0), (0, 4), (0, 80)))
    goal = jnp.pad(targets, ((0, 7), (0, 2), (0, 8))).reshape(80 * 32, 128)
    w = w_in[0]
    wo = jnp.pad(w_out[0], ((0, 7), (0, 0)))
    wo_t = jnp.concatenate([wo.T, wo.T], axis=1)
    vmem = pl.BlockSpec(memory_space=pltpu.VMEM)
    dma = pltpu.SemaphoreType.DMA
    nll, grads = pl.pallas_call(
        kernel,
        out_shape=(
            jax.ShapeDtypeStruct((80 * 32, 128), F32),
            jax.ShapeDtypeStruct((2, 64, 128), F32),
        ),
        in_specs=[vmem] * 13,
        out_specs=(vmem, vmem),
        scratch_shapes=[
            pltpu.VMEM((width * 32, 128), F32),
            pltpu.VMEM((8, width, 512), BF16),
            pltpu.VMEM((width, 32, 128), BF16),
            pltpu.VMEM((own_width, 256, 512), BF16),
            pltpu.VMEM((own_width, 256, 512), BF16),
            pltpu.VMEM((width, 32, 128), BF16),
            pltpu.VMEM((own_width, 256, 512), F32),
            pltpu.VMEM((8, width, 512), F32),
            pltpu.VMEM((8, 80, 512), F32),
            pltpu.VMEM((8, 80, 512), F32),
            pltpu.VMEM((8, 2, 80, 512), F32),
            pltpu.VMEM((own_width, 256, 512), BF16),
            pltpu.VMEM((2, 256, 128), F32),
            pltpu.VMEM((2, 256, 128), F32),
            pltpu.VMEM((4, 2, 64, 128), F32),
            pltpu.VMEM((width, 512), BF16),
            pltpu.VMEM((160, 512), BF16),
            dma((chunks,)),
            dma((chunks,)),
            dma((chunks,)),
            dma((chunks,)),
            dma((chunks,)),
            dma((chunks,)),
            dma,
            dma,
            dma((4,)),
            dma((4,)),
            dma((4,)),
            dma((4,)),
            dma,
            dma,
            dma,
            dma,
        ],
        compiler_params=pltpu.CompilerParams(
            collective_id=0, has_side_effects=True, vmem_limit_bytes=67043328
        ),
    )(
        fields[0], goal, filters, w, w.T, b_in[0][:, None], wo, wo_t,
        jnp.pad(b_out[0], (0, 7))[:, None], lat, lat_t, lon, lon_t,
    )
    nll = nll.reshape(80, 32, 128)[:variables, :own_rows, :own_columns]
    grads = grads[:, :60, :48]
    return nll, grads[0:1], grads[1:2]


def solution(mesh):
    placed = (
        P("member", "lat", "lon", None),
        P(None, "lat", "lon"),
        P("member", "lon", "lat"),
        P("member", "lon", "lat"),
        P("member", None, None),
        P("member", None),
        P("member", None, None),
        P("member", None),
    )
    return jax.shard_map(
        on_device,
        mesh=mesh,
        in_specs=placed,
        out_specs=(P(None, "lat", "lon"), P("member", "lon", "lat"), P("member", "lon", "lat")),
        check_vma=False,
    )
```

time: 504 us -> 297 us (0.59)
  Pallas kernels: 0 us -> 282 us
  waiting for transfers between devices: 184 us -> 0 us
  blocking collectives: 111 us -> 0 us
  local copies, waits for them, and re-layouts: 88.8 us -> 12.3 us
  starting transfers between devices: 40.2 us -> 0 us
  matrix products: 38.7 us -> 0 us
  other arithmetic: 23.8 us -> 1.45 us
  between operations: 15.3 us -> 0.68 us
    pallas_call x0 -> x1, Pallas kernels: none -> 282 us  [on_device(): pl.pallas_call(kernel, out_shape=(jax.ShapeDtypeStruct((80 * 32, 128), F3...]
    all_to_all x3 -> x0, waiting for transfers between devices: 139 us -> none  [the longest x2 139 us: joined_exchange(): lax.all_to_all(blocks, axis, split_axis=0, concat_axis=0, tiled=True)]
    all_to_all x2 -> x0, blocking collectives: 89.6 us -> none  [the longest x1 82.7 us: joined_exchange(): lax.all_to_all(blocks, axis, split_axis=0, concat_axis=0, tiled=True)]
    all_gather x2 -> x0, waiting for transfers between devices: 43.9 us -> none  [sum_by_parts(): whole = lax.all_gather(own, axis, axis=0, tiled=True)]
    dot_general x7 -> x0, matrix products: 38.7 us -> none  [the longest x2 16.1 us: lon_forward(): jnp.einsum('mklc,lq->mkqc', coef, lon_basis, preferred_element_type=jnp.f...]
    all_to_all x3 -> x0, starting transfers between devices: 32 us -> none  [the longest x2 25.6 us: joined_exchange(): lax.all_to_all(blocks, axis, split_axis=0, concat_axis=0, tiled=True)]
    convert_element_type x5 -> x0, local copies, waits for them, and re-layouts: 29.4 us -> none  [the longest x3 22.5 us: on_device(): spatial.astype(jnp.float32)]
    unnamed x1 -> x0, blocking collectives: 21.4 us -> none
  transfers between devices with their start and end apart: 7 -> 0, of which waited for: 5 -> 0; matrix products, arithmetic and copies ran while one was open for 4% -> 0% of each run, Pallas kernels for 0% -> 0%
where the time goes in v1:
time: 297 us; the launch traced here: 296 us
  Pallas kernels  282 us (95%)
  local copies, waits for them, and re-layouts  12.3 us (4%)
    pallas_call x1, Pallas kernels, on_device(): pl.pallas_call(kernel, out_shape=(jax.ShapeDtypeStruct((80 * 32, 128), F3...  282 us

profile of v1, /device:TPU:1, one launch (start us, length us, event | category | flops | bytes accessed | tf_op | source)
XLA Modules:
  0.0 296.4 jit_solution(8503100568927702565)
XLA Ops:
  0.6 0.0 copy-start.1
  0.6 0.0 copy-start
  0.7 0.8 pad_bitcast_fusion
  1.4 0.8 copy.24
  2.2 0.8 copy.25
  3.1 0.7 select_maximum_fusion.filters
  3.7 0.7 copy.31.bo
  4.4 1.0 copy.27
  5.4 0.1 copy.35
  5.6 0.6 pad.18.clone.wo
  6.2 0.8 pad_maximum_fusion.wo_t
  7.0 1.5 copy.29.b
  8.5 0.0 copy-done.1
  8.5 0.9 copy.26
  9.4 0.0 copy-done
  9.4 1.2 pad.16
  10.6 282.0 %shard_map.139 = (f32[2560,128]{1,0:T(8,128)}, f32[2,64,128]{2,1,0:T(8,128)}) custom-call(bf16[30,120,384]{2,1,0:T(8,128)(2,1)} %bitcast.15, f32[2560,128]{1,0:T(8,128)} %bitcast.14, f32[2,64,128]{2,1,0:T(8,128)} %select_maximum_fusion.filters, bf16[384,384]{1,0:T(8,128)(2,1)} %bitcast.16, bf16[384,384]{1,0:T(8,128)(2,1)} %bitcast.17, f32[384,1]{1,0:T(8,128)} %copy.29.b, ...), custom_call_target="tpu_custom_call" | custom-call | tf_op jit(solution)/shard_map/pallas_call | solution.py:370
  292.6 0.0 copy-start.2
  292.6 2.4 slice.15
  295.0 0.0 copy-done.2
  295.0 0.7 copy.33
  295.7 0.7 copy.32
  (2 shorter events, 0.0 us)
Async XLA Ops:
  0.6 7.9 %copy-start.1 = (bf16[1,384,384]{2,1,0:T(8,128)(2,1)S(1)}, bf16[1,384,384]{2,1,0:T(8,128)(2,1)}, u32[]{:S(2)}) copy-start(bf16[1,384,384]{2,1,0:T(8,128)(2,1)} %param.16) | copy-start | bytes 884740
  0.6 8.8 %copy-start = (f32[73,30,120]{2,1,0:T(8,128)S(1)}, f32[73,30,120]{2,1,0:T(8,128)}, u32[]{:S(2)}) copy-start(f32[73,30,120]{2,1,0:T(8,128)} %param.13) | copy-start | bytes 3153604
  292.6 2.4 copy-start.2

commit v2 on v1

v2 whole, which is shorter than its diff:
```python
import functools

import jax
import jax.numpy as jnp
import numpy as np
from jax import lax
from jax.experimental import pallas as pl
from jax.experimental.pallas import tpu as pltpu
from jax.sharding import PartitionSpec as P

MESH_ID = pl.DeviceIdType.MESH
F32 = jnp.float32
BF16 = jnp.bfloat16

rows, columns, width, variables, members = 240, 480, 384, 73, 8
own_rows, own_columns, own_width = 30, 120, 12
chunks = 3
chunk = own_width // chunks
variance_floor = 0.1


def tables():
    k = np.arange(rows, dtype=np.float64)[:, None]
    j = np.arange(rows, dtype=np.float64)[None, :]
    lat = np.where(k == 0, np.sqrt(1.0 / rows), np.sqrt(2.0 / rows)) * np.cos(
        np.pi * k * (j + 0.5) / rows
    )
    half = columns // 2
    place = np.arange(columns, dtype=np.int64)[:, None]
    order = np.arange(half, dtype=np.int64)[None, :]
    angle = 2.0 * np.pi * (place * order % columns).astype(np.float64) / columns
    scale = np.where(order == 0, np.sqrt(1.0 / columns), np.sqrt(2.0 / columns))
    kpad = (np.arange(rows) // 60) * 64 + np.arange(rows) % 60
    jpad = (np.arange(rows) // 30) * 32 + np.arange(rows) % 30
    lpad = (np.arange(columns) // 120) * 128 + np.arange(columns) % 120
    lat_pad = np.zeros((256, 256), np.float32)
    lat_pad[np.ix_(kpad, jpad)] = lat
    lon_pad = np.zeros((512, 512), np.float32)
    lon_pad[np.ix_(lpad, np.arange(half))] = scale * np.cos(angle)
    lon_pad[np.ix_(lpad, 256 + np.arange(half))] = -scale * np.sin(angle)
    return lat_pad, lon_pad


def mm(a, b):
    return jnp.dot(a, b, preferred_element_type=F32)


def wait_for(ref, sem):
    pltpu.make_async_copy(ref, ref, sem).wait()


def kernel(
    fields_hbm, targets_hbm, fre_hbm, fim_hbm, w_hbm, b_hbm, wo_hbm, bo_hbm,
    lat_hbm, lat_t_hbm, lon_hbm, lon_t_hbm,
    nll, grad_re, grad_im,
    fields, targets, fre, fim, w, b, wo, bo, lat, lat_t, lon, lon_t,
    goal, loss_rows, filters, square, w_t, b_col, wo_pad, wo_t, bo_col,
    cells, fields_t, block, grid, spatial, back, spectrum, preact, pred, pred_in, sums, ggrid,
    weights, gsum, gsum_in, mixed, gpair,
    load_sem, out_sem, in_sem, back_out, back_in, gout_sem, gin_sem, pred_out, pred_in_sem,
    sums_out, sums_in, fwd_out, fwd_in, filt_out, filt_in, grad_out, grad_in,
):
    im = lax.axis_index("member")
    ilat = lax.axis_index("lat")
    ilon = lax.axis_index("lon")
    me = ilat * 4 + ilon
    partner = (im // 2) * 2 + 1 - im % 2

    def peer(o):
        y, z = ilat % 4, (ilat // 4) * 4 + ilon
        y2, z2 = (y + o % 4) % 4, (z + o // 4) % 8
        la, lo = (z2 // 4) * 4 + y2, z2 % 4
        return (im, la, lo), la, lo

    def at_member(m):
        return (m, ilat, ilon)

    def load_fields(i):
        part = pl.ds(i * 6, 6)
        return pltpu.make_async_copy(fields_hbm.at[0, part], fields.at[part], load_sem.at[i])

    later = [
        pltpu.make_async_copy(src, dst, load_sem.at[5 + i])
        for i, (src, dst) in enumerate(
            [
                (fre_hbm, fre), (fim_hbm, fim), (lat_hbm, lat), (lon_hbm, lon),
                (lat_t_hbm, lat_t), (lon_t_hbm, lon_t), (w_hbm, w), (b_hbm, b),
                (wo_hbm, wo), (bo_hbm, bo), (targets_hbm, targets),
            ]
        )
    ]
    for i in range(5):
        load_fields(i).start()
    for copy in later:
        copy.start()

    barrier = pltpu.get_barrier_semaphore()

    @pl.loop(1, 32)
    def _(o):
        pl.semaphore_signal(barrier, 1, device_id=peer(o)[0], device_id_type=MESH_ID)

    @pl.loop(1, 8)
    def _(o):
        pl.semaphore_signal(
            barrier, 1, device_id=at_member((im + o) % 8), device_id_type=MESH_ID
        )

    def grid_part(c0, n, la, lo, half=None):
        start, size = (la * 32, 32) if half is None else (la * 32 + half * 16, 16)
        return (
            pl.ds(c0, n),
            pl.ds(pl.multiple_of(start, 16), size),
            pl.ds(pl.multiple_of(lo * 128, 128), 128),
        )

    def block_part(c0, n, la, lo, half=None):
        start, size = (0, 32) if half is None else (half * 16, 16)
        return (pl.ds((la * 4 + lo) * own_width + c0, n), pl.ds(start, size))

    def to_owners(target, c0, n, half, sem_out, sem_in):
        @pl.loop(1, 32)
        def _(o):
            dev, la, lo = peer(o)
            pltpu.make_async_remote_copy(
                block.at[block_part(c0, n, la, lo, half)],
                target.at[grid_part(c0, n, ilat, ilon, half)],
                sem_out,
                sem_in,
                device_id=dev,
                device_id_type=MESH_ID,
            ).start()

        target[grid_part(c0, n, ilat, ilon, half)] = block[block_part(c0, n, ilat, ilon, half)]

    def to_cells(c0, n, half, sem_out, sem_in):
        @pl.loop(1, 32)
        def _(o):
            dev, la, lo = peer(o)
            pltpu.make_async_remote_copy(
                spatial.at[grid_part(c0, n, la, lo, half)],
                back.at[block_part(c0, n, ilat, ilon, half)],
                sem_out,
                sem_in,
                device_id=dev,
                device_id_type=MESH_ID,
            ).start()

        back[block_part(c0, n, ilat, ilon, half)] = spatial[grid_part(c0, n, ilat, ilon, half)]

    def wait_31(n, half, sem):
        size = 32 if half is None else 16
        wait_for(block.at[pl.ds(0, 31 * n), pl.ds(0, size)], sem)

    def turn(j, q):
        x = fields[j].astype(F32)
        x = jnp.concatenate([x, jnp.zeros((8, width), F32)], axis=0).T
        cells[pl.ds(j, width, stride=32), :] = x
        fields_t[j // 4, :, q * 128 : (q + 1) * 128] = x.astype(BF16)

    def fill_block(half):
        @pl.loop(0, width // 8)
        def _(i):
            for c in range(8):
                part = cells[pl.ds(pl.multiple_of(i * 256 + c * 32 + half * 16, 16), 16), :]
                block[i * 8 + c, pl.ds(half * 16, 16), :] = part.astype(BF16)

    for i in range(3):
        load_fields(i).wait()

    @pl.loop(0, 4)
    def _(u):
        for q in range(4):
            turn(u * 4 + q, q)

    fill_block(0)
    pl.semaphore_wait(barrier, 31 + 7)
    to_owners(grid, 0, chunk, 0, out_sem.at[0], in_sem.at[0])

    for i in range(3, 5):
        load_fields(i).wait()

    @pl.loop(4, 7)
    def _(u):
        for q in range(4):
            turn(u * 4 + q, q)

    turn(28, 0)
    turn(29, 1)
    for j in (30, 31):
        cells[pl.ds(j, width, stride=32), :] = jnp.zeros((width, 128), F32)
    fields_t[7, :, 256:512] = jnp.zeros((width, 256), BF16)
    fill_block(1)
    to_owners(grid, 0, chunk, 1, out_sem.at[1], in_sem.at[1])
    for ch in range(1, chunks):
        to_owners(grid, ch * chunk, chunk, None, out_sem.at[ch + 1], in_sem.at[ch + 1])

    for copy in later:
        copy.wait()
    for n, part in enumerate((fre, fim)):
        square[...] = jnp.zeros_like(square)
        square[0:48, 0:60] = part[0]
        filters[n] = square[...].T[0:64]

    @pl.loop(1, 4)
    def _(o):
        pltpu.make_async_remote_copy(
            filters,
            weights.at[:, pl.ds(pl.multiple_of(ilon * 64, 64), 64), :],
            filt_out,
            filt_in,
            device_id=(im, ilat, (ilon + o) % 4),
            device_id_type=MESH_ID,
        ).start()

    weights[:, pl.ds(pl.multiple_of(ilon * 64, 64), 64), :] = filters[...]

    w_t[...] = w[0].astype(F32).T.astype(BF16)
    b_col[...] = jnp.broadcast_to(b[...], (128, width)).T
    wo_pad[...] = jnp.zeros_like(wo_pad)
    wo_pad[0:variables, :] = wo[0].astype(F32)
    turned = wo_pad[...].T.astype(BF16)
    wo_t[:, 0:128] = turned
    wo_t[:, 128:256] = turned
    bo_col[...] = jnp.zeros_like(bo_col)
    bo_col[0:1, 0:variables] = bo[...]
    bo_col[...] = jnp.broadcast_to(bo_col[0:1, :], (128, 128)).T
    goal[...] = jnp.zeros_like(goal)

    @pl.loop(0, variables)
    def _(v):
        goal[pl.ds(pl.multiple_of(v * 32, 32), own_rows), 0:own_columns] = targets[v]

    gpair[...] = jnp.zeros_like(gpair)
    gsum[...] = jnp.zeros_like(gsum)
    wait_for(weights.at[:, pl.ds(0, 192), :], filt_in)

    lane = lax.broadcasted_iota(jnp.int32, (256, 128), 1)
    k_row = lax.broadcasted_iota(jnp.int32, (256, 256), 0)
    keep = (k_row // 64) * 60 + k_row % 64 >= lax.broadcasted_iota(jnp.int32, (256, 256), 1)

    def to_spectral(x):
        return mm(mm(lat[...], x).astype(BF16), lon[...])

    for ch in range(chunks):
        if ch == 0:
            wait_31(chunk, 0, in_sem.at[0])
            wait_31(chunk, 1, in_sem.at[1])
        else:
            wait_31(chunk, None, in_sem.at[ch + 1])

        @pl.loop(ch * chunk, (ch + 1) * chunk)
        def _(c):
            own = lane == ilon * own_width + c
            wr = jnp.sum(jnp.where(own, weights[0], 0.0), axis=1, keepdims=True)
            wi = jnp.sum(jnp.where(own, weights[1], 0.0), axis=1, keepdims=True)
            spectrum[c] = to_spectral(grid[c])
            sr, si = spectrum[c, :, 0:256], spectrum[c, :, 256:512]
            fr = jnp.where(keep, wr * sr - wi * si, 0.0).astype(BF16)
            fi = jnp.where(keep, wr * si + wi * sr, 0.0).astype(BF16)
            lon_back = mm(jnp.concatenate([fr, fi], axis=1), lon_t[...]).astype(BF16)
            spatial[c] = mm(lat_t[...], lon_back).astype(BF16)

        if ch < chunks - 1:
            to_cells(ch * chunk, chunk, None, back_out.at[ch], back_in.at[ch])
        else:
            to_cells(ch * chunk, chunk, 0, back_out.at[ch], back_in.at[ch])
            to_cells(ch * chunk, chunk, 1, back_out.at[ch + 1], back_in.at[ch + 1])

    def unpack(ch, half):
        @pl.loop(0, 32)
        def _(s):
            first = s * own_width + ch * chunk
            for c in range(chunk):
                rows_at = pl.multiple_of((first + c) * 32 + half * 16, 16)
                part = back[first + c, pl.ds(half * 16, 16), :]
                cells[pl.ds(rows_at, 16), :] = part.astype(F32)

    def decode(half, i):
        u = half * 4 + i
        for q in range(4):
            part = fields_t[u, :, q * 128 : (q + 1) * 128].astype(F32)
            part = part + cells[pl.ds(4 * u + q, width, stride=32), :]
            mixed[:, q * 128 : (q + 1) * 128] = part.astype(BF16)
        bias = b_col[...]
        pa = mm(w_t[...], mixed[...]) + jnp.concatenate([bias] * 4, axis=1)
        preact[u] = pa
        hidden = (pa / (1.0 + jnp.exp(-pa))).astype(BF16)
        bias = bo_col[0:80, :]
        out = mm(wo_pad[0:80, :].astype(BF16), hidden) + jnp.concatenate([bias] * 4, axis=1)
        pred[half, 2 * i] = out[:, 0:256]
        pred[half, 2 * i + 1] = out[:, 256:512]

    def decode_half(half):
        @pl.loop(0, 4)
        def _(o):
            i = (im // 2 + 1 + o) % 4
            decode(half, i)
            for e in range(2):
                r = 2 * i + e

                @pl.when(r != im)
                def _():
                    pltpu.make_async_remote_copy(
                        pred.at[half, r],
                        pred_in.at[half, im],
                        pred_out.at[half],
                        pred_in_sem.at[half],
                        device_id=at_member(r),
                        device_id_type=MESH_ID,
                    ).start()

    def sums_copy(half, index, m, sem_out, sem_in):
        return pltpu.make_async_remote_copy(
            sums.at[half, index],
            sums.at[half, index],
            sem_out,
            sem_in,
            device_id=at_member(m),
            device_id_type=MESH_ID,
        )

    def sum_half(half):
        pred_in[half, im] = pred[half, im]
        wait_for(pred.at[half, pl.ds(0, 7)], pred_in_sem.at[half])
        first = pred_in[half, 0]
        second = first * first
        for s in range(1, members):
            one = pred_in[half, s]
            first = first + one
            second = second + one * one
        sums[half, im, 0] = first
        sums[half, im, 1] = second
        for t in (1, 2, 3):
            sums_copy(
                half, im, (im + 2 * t) % 8, sums_out.at[half, t], sums_in.at[half, t]
            ).start()
        sums_copy(half, im, partner, sums_out.at[half, 0], sums_in.at[half, 0]).start()

    def backward(half, i):
        u = half * 4 + i
        mean, var = [
            jnp.concatenate([sums[half, 2 * i, n], sums[half, 2 * i + 1, n]], axis=1) / members
            for n in range(2)
        ]
        own_pred = jnp.concatenate([pred[half, 2 * i], pred[half, 2 * i + 1]], axis=1)
        var = var - mean * mean + variance_floor
        want = jnp.concatenate(
            [goal[pl.ds(4 * u + q, 80, stride=32), :] for q in range(4)], axis=1
        )
        res = want - mean
        inv = 1.0 / var
        loss = 0.5 * (jnp.log(var) + res * res * inv)
        for q in range(4):
            loss_rows[pl.ds(4 * u + q, 80, stride=32), :] = loss[:, q * 128 : (q + 1) * 128]
        gp = (
            -res * inv / members
            + (inv - res * res * inv * inv) * (own_pred - mean) / members
        ) / variables
        high = gp.astype(BF16)
        gpair[0:80, :] = high
        gpair[128:208, :] = (gp - high.astype(F32)).astype(BF16)
        gh = mm(wo_t[...], gpair[...])
        pa = preact[u]
        sg = 1.0 / (1.0 + jnp.exp(-pa))
        gpre = (gh * sg * (1.0 + pa * (1.0 - sg))).astype(BF16)
        gm = mm(w[0], gpre)
        for q in range(4):
            cells[pl.ds(4 * u + q, width, stride=32), :] = gm[:, q * 128 : (q + 1) * 128]

    def backward_half(half):
        wait_for(sums.at[half, 0], sums_in.at[half, 0])
        backward(half, im // 2)
        for t in (1, 2, 3):
            wait_for(sums.at[half, 0], sums_in.at[half, t])
            sums_copy(
                half, (im + 8 - 2 * t) % 8, partner, fwd_out.at[half, t], fwd_in.at[half, t]
            ).start()

        @pl.loop(1, 4)
        def _(t):
            wait_for(sums.at[half, 0], fwd_in.at[half, t])
            backward(half, (im // 2 + 4 - t) % 4)

    for ch in range(chunks):
        wait_31(chunk, None if ch < chunks - 1 else 0, back_in.at[ch])
        unpack(ch, 0)
    decode_half(0)
    for ch in range(chunks - 1):
        unpack(ch, 1)
    sum_half(0)
    wait_31(chunk, 1, back_in.at[chunks])
    unpack(chunks - 1, 1)
    decode_half(1)
    wait_31(chunk, 0, out_sem.at[0])
    wait_31(chunk, 1, out_sem.at[1])
    for ch in range(1, chunks):
        wait_31(chunk, None, out_sem.at[ch + 1])
    backward_half(0)
    fill_block(0)
    to_owners(ggrid, 0, own_width, 0, gout_sem.at[chunks], gin_sem.at[chunks])
    sum_half(1)
    backward_half(1)
    fill_block(1)
    for ch in range(chunks):
        to_owners(ggrid, ch * chunk, chunk, 1, gout_sem.at[ch], gin_sem.at[ch])

    @pl.loop(0, variables)
    def _(v):
        nll[v] = loss_rows[pl.ds(pl.multiple_of(v * 32, 32), own_rows), 0:own_columns]

    wait_31(own_width, 0, gin_sem.at[chunks])
    for ch in range(chunks):
        wait_31(chunk, 1, gin_sem.at[ch])

        @pl.loop(ch * chunk, (ch + 1) * chunk)
        def _(c):
            own = lane == ilon * own_width + c
            g = to_spectral(ggrid[c])
            gr, gi = g[:, 0:256], g[:, 256:512]
            sr, si = spectrum[c, :, 0:256], spectrum[c, :, 256:512]
            g_re = jnp.sum(jnp.where(keep, gr * sr + gi * si, 0.0), axis=1, keepdims=True)
            g_im = jnp.sum(jnp.where(keep, gi * sr - gr * si, 0.0), axis=1, keepdims=True)
            gsum[0] = gsum[0] + jnp.where(own, g_re, 0.0)
            gsum[1] = gsum[1] + jnp.where(own, g_im, 0.0)

    @pl.loop(1, 4)
    def _(o):
        lo = (ilon + o) % 4
        pltpu.make_async_remote_copy(
            gsum.at[:, pl.ds(pl.multiple_of(lo * 64, 64), 64), :],
            gsum_in.at[ilon],
            grad_out,
            grad_in,
            device_id=(im, ilat, lo),
            device_id_type=MESH_ID,
        ).start()

    gsum_in[ilon] = gsum[:, pl.ds(pl.multiple_of(ilon * 64, 64), 64), :]
    wait_for(gsum_in.at[pl.ds(0, 3)], grad_in)
    total = gsum_in[0] + gsum_in[1] + gsum_in[2] + gsum_in[3]
    for n, part in enumerate((grad_re, grad_im)):
        square[0:64] = total[n]
        part[0] = square[...].T[0:48, 0:60]

    for ch in range(chunks - 1):
        wait_31(chunk, None, back_out.at[ch])
    wait_31(chunk, 0, back_out.at[chunks - 1])
    wait_31(chunk, 1, back_out.at[chunks])
    wait_31(own_width, 0, gout_sem.at[chunks])
    for ch in range(chunks):
        wait_31(chunk, 1, gout_sem.at[ch])
    for half in range(2):
        wait_for(pred.at[half, pl.ds(0, 7)], pred_out.at[half])
        for t in range(4):
            wait_for(sums.at[half, 0], sums_out.at[half, t])
        for t in (1, 2, 3):
            wait_for(sums.at[half, 0], fwd_out.at[half, t])
    wait_for(weights.at[:, pl.ds(0, 192), :], filt_out)
    wait_for(gsum_in.at[pl.ds(0, 3)], grad_out)


def on_device(fields, targets, filt_re, filt_im, w_in, b_in, w_out, b_out):
    lat_pad, lon_pad = tables()
    lat = jnp.asarray(lat_pad, BF16)
    lat_t = jnp.asarray(lat_pad.T.copy(), BF16)
    lon = jnp.asarray(lon_pad, BF16)
    lon_t = jnp.asarray(lon_pad.T.copy(), BF16)
    anywhere = pl.BlockSpec(memory_space=pl.ANY)
    vmem = pl.BlockSpec(memory_space=pltpu.VMEM)
    dma = pltpu.SemaphoreType.DMA
    filt_re, filt_im = jnp.swapaxes(filt_re, 1, 2), jnp.swapaxes(filt_im, 1, 2)
    nll, grad_re, grad_im = pl.pallas_call(
        kernel,
        out_shape=(
            jax.ShapeDtypeStruct(targets.shape, F32),
            jax.ShapeDtypeStruct(filt_re.shape, F32),
            jax.ShapeDtypeStruct(filt_re.shape, F32),
        ),
        in_specs=[anywhere] * 12,
        out_specs=(vmem, vmem, vmem),
        scratch_shapes=[
            pltpu.VMEM(fields.shape[1:], BF16),
            pltpu.VMEM(targets.shape, F32),
            pltpu.VMEM(filt_re.shape, F32),
            pltpu.VMEM(filt_im.shape, F32),
            pltpu.VMEM(w_in.shape, BF16),
            pltpu.VMEM(b_in.shape, F32),
            pltpu.VMEM(w_out.shape, BF16),
            pltpu.VMEM(b_out.shape, F32),
            pltpu.VMEM((256, 256), BF16),
            pltpu.VMEM((256, 256), BF16),
            pltpu.VMEM((512, 512), BF16),
            pltpu.VMEM((512, 512), BF16),
            pltpu.VMEM((80 * 32, 128), F32),
            pltpu.VMEM((80 * 32, 128), F32),
            pltpu.VMEM((2, 64, 128), F32),
            pltpu.VMEM((128, 128), F32),
            pltpu.VMEM((width, width), BF16),
            pltpu.VMEM((width, 128), F32),
            pltpu.VMEM((128, width), F32),
            pltpu.VMEM((width, 256), BF16),
            pltpu.VMEM((128, 128), F32),
            pltpu.VMEM((width * 32, 128), F32),
            pltpu.VMEM((8, width, 512), BF16),
            pltpu.VMEM((width, 32, 128), BF16),
            pltpu.VMEM((own_width, 256, 512), BF16),
            pltpu.VMEM((own_width, 256, 512), BF16),
            pltpu.VMEM((width, 32, 128), BF16),
            pltpu.VMEM((own_width, 256, 512), F32),
            pltpu.VMEM((8, width, 512), F32),
            pltpu.VMEM((2, 8, 80, 256), F32),
            pltpu.VMEM((2, 8, 80, 256), F32),
            pltpu.VMEM((2, 8, 2, 80, 256), F32),
            pltpu.VMEM((own_width, 256, 512), BF16),
            pltpu.VMEM((2, 256, 128), F32),
            pltpu.VMEM((2, 256, 128), F32),
            pltpu.VMEM((4, 2, 64, 128), F32),
            pltpu.VMEM((width, 512), BF16),
            pltpu.VMEM((256, 512), BF16),
            dma((16,)),
            dma((chunks + 1,)),
            dma((chunks + 1,)),
            dma((chunks + 1,)),
            dma((chunks + 1,)),
            dma((chunks + 1,)),
            dma((chunks + 1,)),
            dma((2,)),
            dma((2,)),
            dma((2, 4)),
            dma((2, 4)),
            dma((2, 4)),
            dma((2, 4)),
            dma,
            dma,
            dma,
            dma,
        ],
        compiler_params=pltpu.CompilerParams(
            collective_id=0, has_side_effects=True, vmem_limit_bytes=67043328
        ),
    )(fields, targets, filt_re, filt_im, w_in, b_in, w_out, b_out, lat, lat_t, lon, lon_t)
    return nll, jnp.swapaxes(grad_re, 1, 2), jnp.swapaxes(grad_im, 1, 2)


def solution(mesh):
    placed = (
        P("member", "lat", "lon", None),
        P(None, "lat", "lon"),
        P("member", "lon", "lat"),
        P("member", "lon", "lat"),
        P("member", None, None),
        P("member", None),
        P("member", None, None),
        P("member", None),
    )
    return jax.shard_map(
        on_device,
        mesh=mesh,
        in_specs=placed,
        out_specs=(P(None, "lat", "lon"), P("member", "lon", "lat"), P("member", "lon", "lat")),
        check_vma=False,
    )
```

time: 297 us -> 261 us (0.88)
  Pallas kernels: 282 us -> 255 us
  local copies, waits for them, and re-layouts: 12.3 us -> 3.61 us
    pallas_call x1, Pallas kernels: 282 us -> 255 us  [on_device(): pl.pallas_call(kernel, out_shape=(jax.ShapeDtypeStruct(targets.shape, F32...]
where the time goes in v2:
time: 261 us; the launch traced here: 260 us
  Pallas kernels  255 us (98%)
  local copies, waits for them, and re-layouts  3.61 us (1%)
    pallas_call x1, Pallas kernels, on_device(): pl.pallas_call(kernel, out_shape=(jax.ShapeDtypeStruct(targets.shape, F32...  255 us

profile of v2, /device:TPU:1, one launch (start us, length us, event | category | flops | bytes accessed | tf_op | source)
XLA Modules:
  0.0 259.6 jit_solution(390164080253930209)
XLA Ops:
  0.6 255.3 %shard_map.139 = (f32[73,30,120]{2,1,0:T(8,128)}, f32[1,48,60]{2,1,0:T(8,128)}, f32[1,48,60]{2,1,0:T(8,128)}) custom-call(bf16[1,30,120,384]{3,2,1,0:T(8,128)(2,1)} %fields_hbm.1, f32[73,30,120]{2,1,0:T(8,128)} %targets_hbm.1, f32[1,48,60]{2,1,0:T(8,128)} %bitcast.6, f32[1,48,60]{2,1,0:T(8,128)} %bitcast.7, bf16[1,384,384]{2,1,0:T(8,128)(2,1)} %w_hbm.1, ...), custom_call_target="tpu_custom_call" | custom-call | tf_op jit(solution)/shard_map/pallas_call | solution.py:473
  256.0 0.0 copy-start.1
  256.0 0.0 copy-start
  256.0 2.4 copy.18
  258.4 0.0 copy-done.1
  258.4 0.6 copy.19
  259.0 0.0 copy-done
  259.0 0.6 copy.20
Async XLA Ops:
  256.0 2.4 copy-start.1
  256.0 3.0 %copy-start = (f32[1,48,60]{2,1,0:T(8,128)S(1)}, f32[1,48,60]{2,1,0:T(8,128)}, u32[]{:S(2)}) copy-start(f32[1,48,60]{2,1,0:T(8,128)} %get-tuple-element.8) | copy-start | bytes 34564

commit v3 on v2

--- a/solution.py
+++ b/solution.py
@@ -14,6 +14,7 @@
 
 rows, columns, width, variables, members = 240, 480, 384, 73, 8
 own_rows, own_columns, own_width = 30, 120, 12
+low = 14
 chunks = 3
 chunk = own_width // chunks
 variance_floor = 0.1
@@ -31,7 +32,8 @@
     angle = 2.0 * np.pi * (place * order % columns).astype(np.float64) / columns
     scale = np.where(order == 0, np.sqrt(1.0 / columns), np.sqrt(2.0 / columns))
     kpad = (np.arange(rows) // 60) * 64 + np.arange(rows) % 60
-    jpad = (np.arange(rows) // 30) * 32 + np.arange(rows) % 30
+    part, inside = np.arange(rows) // 30, np.arange(rows) % 30
+    jpad = np.where(inside < 16, part * 16 + inside, 128 + part * 16 + inside - 16)
     lpad = (np.arange(columns) // 120) * 128 + np.arange(columns) % 120
     lat_pad = np.zeros((256, 256), np.float32)
     lat_pad[np.ix_(kpad, jpad)] = lat
@@ -55,9 +57,10 @@
     nll, grad_re, grad_im,
     fields, targets, fre, fim, w, b, wo, bo, lat, lat_t, lon, lon_t,
     goal, loss_rows, filters, square, w_t, b_col, wo_pad, wo_t, bo_col,
-    cells, fields_t, block, grid, spatial, back, spectrum, preact, pred, pred_in, sums, ggrid,
+    cells, fields_t, block, block_low, grid, grid_low, spatial, spatial_low, back, back_low,
+    spectrum, preact, pred, pred_in, sums, ggrid, ggrid_low, line, nll_all,
     weights, gsum, gsum_in, mixed, gpair,
-    load_sem, out_sem, in_sem, back_out, back_in, gout_sem, gin_sem, pred_out, pred_in_sem,
+    load_sem, nll_sem, out_sem, in_sem, back_out, back_in, gout_sem, gin_sem, pred_out, pred_in_sem,
     sums_out, sums_in, fwd_out, fwd_in, filt_out, filt_in, grad_out, grad_in,
 ):
     im = lax.axis_index("member")
@@ -106,51 +109,45 @@
             barrier, 1, device_id=at_member((im + o) % 8), device_id_type=MESH_ID
         )
 
-    def grid_part(c0, n, la, lo, half=None):
-        start, size = (la * 32, 32) if half is None else (la * 32 + half * 16, 16)
+    def grid_part(c0, n, la, lo):
         return (
             pl.ds(c0, n),
-            pl.ds(pl.multiple_of(start, 16), size),
+            pl.ds(pl.multiple_of(la * 16, 16), 16),
             pl.ds(pl.multiple_of(lo * 128, 128), 128),
         )
 
-    def block_part(c0, n, la, lo, half=None):
-        start, size = (0, 32) if half is None else (half * 16, 16)
-        return (pl.ds((la * 4 + lo) * own_width + c0, n), pl.ds(start, size))
-
-    def to_owners(target, c0, n, half, sem_out, sem_in):
+    def block_part(c0, n, la, lo):
+        return (pl.ds((la * 4 + lo) * own_width + c0, n),)
+
+    def low_part(c0, n, la, lo):
+        return (la * 4 + lo, pl.ds(c0 * low, n * low))
+
+    def exchange(src, src_part, dst, dst_part, c0, n, sem_out, sem_in):
         @pl.loop(1, 32)
         def _(o):
             dev, la, lo = peer(o)
             pltpu.make_async_remote_copy(
-                block.at[block_part(c0, n, la, lo, half)],
-                target.at[grid_part(c0, n, ilat, ilon, half)],
+                src.at[src_part(c0, n, la, lo)],
+                dst.at[dst_part(c0, n, ilat, ilon)],
                 sem_out,
                 sem_in,
                 device_id=dev,
                 device_id_type=MESH_ID,
             ).start()
 
-        target[grid_part(c0, n, ilat, ilon, half)] = block[block_part(c0, n, ilat, ilon, half)]
-
-    def to_cells(c0, n, half, sem_out, sem_in):
-        @pl.loop(1, 32)
-        def _(o):
-            dev, la, lo = peer(o)
-            pltpu.make_async_remote_copy(
-                spatial.at[grid_part(c0, n, la, lo, half)],
-                back.at[block_part(c0, n, ilat, ilon, half)],
-                sem_out,
-                sem_in,
-                device_id=dev,
-                device_id_type=MESH_ID,
-            ).start()
-
-        back[block_part(c0, n, ilat, ilon, half)] = spatial[grid_part(c0, n, ilat, ilon, half)]
-
-    def wait_31(n, half, sem):
-        size = 32 if half is None else 16
-        wait_for(block.at[pl.ds(0, 31 * n), pl.ds(0, size)], sem)
+        dst[dst_part(c0, n, ilat, ilon)] = src[src_part(c0, n, ilat, ilon)]
+
+    def to_owners(target, c0, n, sem_out, sem_in):
+        exchange(block, block_part, target, grid_part, c0, n, sem_out, sem_in)
+
+    def low_to_owners(target, c0, n, sem_out, sem_in):
+        exchange(block_low, low_part, target, low_part, c0, n, sem_out, sem_in)
+
+    def wait_31(n, sem):
+        wait_for(block.at[pl.ds(0, 31 * n)], sem)
+
+    def wait_low(n, sem):
+        wait_for(block_low.at[pl.ds(0, 31), pl.ds(0, n * low)], sem)
 
     def turn(j, q):
         x = fields[j].astype(F32)
@@ -158,12 +155,37 @@
         cells[pl.ds(j, width, stride=32), :] = x
         fields_t[j // 4, :, q * 128 : (q + 1) * 128] = x.astype(BF16)
 
-    def fill_block(half):
+    def fill_block():
         @pl.loop(0, width // 8)
         def _(i):
             for c in range(8):
-                part = cells[pl.ds(pl.multiple_of(i * 256 + c * 32 + half * 16, 16), 16), :]
-                block[i * 8 + c, pl.ds(half * 16, 16), :] = part.astype(BF16)
+                part = cells[pl.ds(pl.multiple_of(i * 256 + c * 32, 32), 16), :]
+                block[i * 8 + c] = part.astype(BF16)
+
+    def fill_low():
+        @pl.loop(0, 16)
+        def _(i):
+            for e in range(2):
+                d = i * 2 + e
+                for c in range(own_width):
+                    first = pl.multiple_of((d * own_width + c) * 32 + 16, 16)
+                    line[e, pl.ds(c * low, 16), :] = cells[pl.ds(first, 16), :]
+                block_low[d] = line[e, 0 : own_width * low, :].astype(BF16)
+
+    def spread_low(src, target, ch):
+        @pl.loop(0, 8)
+        def _(la):
+            for lo in range(4):
+                part = src[la * 4 + lo, pl.ds(ch * chunk * low, chunk * low)]
+                line[lo, 0 : chunk * low, :] = part.astype(F32)
+                for c in range(chunk):
+                    target[
+                        ch * chunk + c,
+                        pl.ds(pl.multiple_of(128 + la * 16, 16), 16),
+                        lo * 128 : (lo + 1) * 128,
+                    ] = line[lo, pl.ds(c * low, 16), :].astype(BF16)
+
+    line[...] = jnp.zeros_like(line)
 
     for i in range(3):
         load_fields(i).wait()
@@ -173,34 +195,16 @@
         for q in range(4):
             turn(u * 4 + q, q)
 
-    fill_block(0)
-    pl.semaphore_wait(barrier, 31 + 7)
-    to_owners(grid, 0, chunk, 0, out_sem.at[0], in_sem.at[0])
-
-    for i in range(3, 5):
-        load_fields(i).wait()
-
-    @pl.loop(4, 7)
-    def _(u):
-        for q in range(4):
-            turn(u * 4 + q, q)
-
-    turn(28, 0)
-    turn(29, 1)
-    for j in (30, 31):
-        cells[pl.ds(j, width, stride=32), :] = jnp.zeros((width, 128), F32)
-    fields_t[7, :, 256:512] = jnp.zeros((width, 256), BF16)
-    fill_block(1)
-    to_owners(grid, 0, chunk, 1, out_sem.at[1], in_sem.at[1])
-    for ch in range(1, chunks):
-        to_owners(grid, ch * chunk, chunk, None, out_sem.at[ch + 1], in_sem.at[ch + 1])
-
-    for copy in later:
+    fill_block()
+
+    for copy in later[:2]:
         copy.wait()
     for n, part in enumerate((fre, fim)):
         square[...] = jnp.zeros_like(square)
         square[0:48, 0:60] = part[0]
         filters[n] = square[...].T[0:64]
+
+    pl.semaphore_wait(barrier, 31 + 7)
 
     @pl.loop(1, 4)
     def _(o):
@@ -214,6 +218,32 @@
         ).start()
 
     weights[:, pl.ds(pl.multiple_of(ilon * 64, 64), 64), :] = filters[...]
+
+    to_owners(grid, 0, chunk, out_sem.at[0], in_sem.at[0])
+
+    for i in range(3, 5):
+        load_fields(i).wait()
+
+    @pl.loop(4, 7)
+    def _(u):
+        for q in range(4):
+            turn(u * 4 + q, q)
+
+    turn(28, 0)
+    turn(29, 1)
+    for j in (30, 31):
+        cells[pl.ds(j, width, stride=32), :] = jnp.zeros((width, 128), F32)
+    fields_t[7, :, 256:512] = jnp.zeros((width, 256), BF16)
+    fill_low()
+    for ch in range(chunks):
+        if ch > 0:
+            to_owners(grid, ch * chunk, chunk, out_sem.at[ch], in_sem.at[ch])
+        low_to_owners(
+            grid_low, ch * chunk, chunk, out_sem.at[chunks + ch], in_sem.at[chunks + ch]
+        )
+
+    for copy in later[2:]:
+        copy.wait()
 
     w_t[...] = w[0].astype(F32).T.astype(BF16)
     b_col[...] = jnp.broadcast_to(b[...], (128, width)).T
@@ -243,11 +273,9 @@
         return mm(mm(lat[...], x).astype(BF16), lon[...])
 
     for ch in range(chunks):
-        if ch == 0:
-            wait_31(chunk, 0, in_sem.at[0])
-            wait_31(chunk, 1, in_sem.at[1])
-        else:
-            wait_31(chunk, None, in_sem.at[ch + 1])
+        wait_31(chunk, in_sem.at[ch])
+        wait_low(chunk, in_sem.at[chunks + ch])
+        spread_low(grid_low, grid, ch)
 
         @pl.loop(ch * chunk, (ch + 1) * chunk)
         def _(c):
@@ -259,22 +287,44 @@
             fr = jnp.where(keep, wr * sr - wi * si, 0.0).astype(BF16)
             fi = jnp.where(keep, wr * si + wi * sr, 0.0).astype(BF16)
             lon_back = mm(jnp.concatenate([fr, fi], axis=1), lon_t[...]).astype(BF16)
-            spatial[c] = mm(lat_t[...], lon_back).astype(BF16)
-
-        if ch < chunks - 1:
-            to_cells(ch * chunk, chunk, None, back_out.at[ch], back_in.at[ch])
-        else:
-            to_cells(ch * chunk, chunk, 0, back_out.at[ch], back_in.at[ch])
-            to_cells(ch * chunk, chunk, 1, back_out.at[ch + 1], back_in.at[ch + 1])
-
-    def unpack(ch, half):
+            spatial[c] = mm(lat_t[0:128, :], lon_back).astype(BF16)
+            rest = mm(lat_t[128:256, :], lon_back)
+            for la in range(8):
+                for lo in range(4):
+                    cells[pl.ds((la * 4 + lo) * 176 + c * low, 16), :] = rest[
+                        la * 16 : la * 16 + 16, lo * 128 : lo * 128 + 128
+                    ]
+
+        exchange(
+            spatial, grid_part, back, block_part, ch * chunk, chunk, back_out.at[ch], back_in.at[ch]
+        )
+
+    @pl.loop(0, 32)
+    def _(d):
+        part = cells[pl.ds(pl.multiple_of(d * 176, 16), own_width * low), :]
+        spatial_low[d] = part.astype(BF16)
+
+    exchange(
+        spatial_low, low_part, back_low, low_part, 0, own_width,
+        back_out.at[chunks], back_in.at[chunks],
+    )
+
+    def unpack(ch):
         @pl.loop(0, 32)
         def _(s):
             first = s * own_width + ch * chunk
             for c in range(chunk):
-                rows_at = pl.multiple_of((first + c) * 32 + half * 16, 16)
-                part = back[first + c, pl.ds(half * 16, 16), :]
-                cells[pl.ds(rows_at, 16), :] = part.astype(F32)
+                cells[pl.ds(pl.multiple_of((first + c) * 32, 32), 16), :] = back[first + c].astype(F32)
+
+    def unpack_low():
+        @pl.loop(0, 16)
+        def _(i):
+            for e in range(2):
+                s = i * 2 + e
+                line[e, 0 : own_width * low, :] = back_low[s].astype(F32)
+                for c in range(own_width):
+                    first = pl.multiple_of((s * own_width + c) * 32 + 16, 16)
+                    cells[pl.ds(first, 16), :] = line[e, pl.ds(c * low, 16), :]
 
     def decode(half, i):
         u = half * 4 + i
@@ -383,35 +433,35 @@
             backward(half, (im // 2 + 4 - t) % 4)
 
     for ch in range(chunks):
-        wait_31(chunk, None if ch < chunks - 1 else 0, back_in.at[ch])
-        unpack(ch, 0)
+        wait_31(chunk, back_in.at[ch])
+        unpack(ch)
     decode_half(0)
-    for ch in range(chunks - 1):
-        unpack(ch, 1)
+    for ch in range(chunks):
+        wait_31(chunk, out_sem.at[ch])
+        wait_low(chunk, out_sem.at[chunks + ch])
     sum_half(0)
-    wait_31(chunk, 1, back_in.at[chunks])
-    unpack(chunks - 1, 1)
+    backward_half(0)
+    fill_block()
+    to_owners(ggrid, 0, own_width, gout_sem.at[chunks], gin_sem.at[chunks])
+    wait_low(own_width, back_in.at[chunks])
+    unpack_low()
     decode_half(1)
-    wait_31(chunk, 0, out_sem.at[0])
-    wait_31(chunk, 1, out_sem.at[1])
-    for ch in range(1, chunks):
-        wait_31(chunk, None, out_sem.at[ch + 1])
-    backward_half(0)
-    fill_block(0)
-    to_owners(ggrid, 0, own_width, 0, gout_sem.at[chunks], gin_sem.at[chunks])
     sum_half(1)
     backward_half(1)
-    fill_block(1)
-    for ch in range(chunks):
-        to_owners(ggrid, ch * chunk, chunk, 1, gout_sem.at[ch], gin_sem.at[ch])
+    fill_low()
+    for ch in range(chunks):
+        low_to_owners(ggrid_low, ch * chunk, chunk, gout_sem.at[ch], gin_sem.at[ch])
 
     @pl.loop(0, variables)
     def _(v):
-        nll[v] = loss_rows[pl.ds(pl.multiple_of(v * 32, 32), own_rows), 0:own_columns]
-
-    wait_31(own_width, 0, gin_sem.at[chunks])
-    for ch in range(chunks):
-        wait_31(chunk, 1, gin_sem.at[ch])
+        nll_all[v] = loss_rows[pl.ds(pl.multiple_of(v * 32, 32), own_rows), 0:own_columns]
+
+    nll_copy = pltpu.make_async_copy(nll_all, nll, nll_sem)
+    nll_copy.start()
+    wait_31(own_width, gin_sem.at[chunks])
+    for ch in range(chunks):
+        wait_low(chunk, gin_sem.at[ch])
+        spread_low(ggrid_low, ggrid, ch)
 
         @pl.loop(ch * chunk, (ch + 1) * chunk)
         def _(c):
@@ -443,13 +493,13 @@
         square[0:64] = total[n]
         part[0] = square[...].T[0:48, 0:60]
 
-    for ch in range(chunks - 1):
-        wait_31(chunk, None, back_out.at[ch])
-    wait_31(chunk, 0, back_out.at[chunks - 1])
-    wait_31(chunk, 1, back_out.at[chunks])
-    wait_31(own_width, 0, gout_sem.at[chunks])
-    for ch in range(chunks):
-        wait_31(chunk, 1, gout_sem.at[ch])
+    for ch in range(chunks):
+        wait_31(chunk, back_out.at[ch])
+    wait_low(own_width, back_out.at[chunks])
+    wait_31(own_width, gout_sem.at[chunks])
+    for ch in range(chunks):
+        wait_low(chunk, gout_sem.at[ch])
+    nll_copy.wait()
     for half in range(2):
         wait_for(pred.at[half, pl.ds(0, 7)], pred_out.at[half])
         for t in range(4):
@@ -478,7 +528,7 @@
             jax.ShapeDtypeStruct(filt_re.shape, F32),
         ),
         in_specs=[anywhere] * 12,
-        out_specs=(vmem, vmem, vmem),
+        out_specs=(anywhere, vmem, vmem),
         scratch_shapes=[
             pltpu.VMEM(fields.shape[1:], BF16),
             pltpu.VMEM(targets.shape, F32),
@@ -503,24 +553,32 @@
             pltpu.VMEM((128, 128), F32),
             pltpu.VMEM((width * 32, 128), F32),
             pltpu.VMEM((8, width, 512), BF16),
-            pltpu.VMEM((width, 32, 128), BF16),
+            pltpu.VMEM((width, 16, 128), BF16),
+            pltpu.VMEM((32, own_width * low, 128), BF16),
             pltpu.VMEM((own_width, 256, 512), BF16),
-            pltpu.VMEM((own_width, 256, 512), BF16),
-            pltpu.VMEM((width, 32, 128), BF16),
+            pltpu.VMEM((32, own_width * low, 128), BF16),
+            pltpu.VMEM((own_width, 128, 512), BF16),
+            pltpu.VMEM((32, own_width * low, 128), BF16),
+            pltpu.VMEM((width, 16, 128), BF16),
+            pltpu.VMEM((32, own_width * low, 128), BF16),
             pltpu.VMEM((own_width, 256, 512), F32),
             pltpu.VMEM((8, width, 512), F32),
             pltpu.VMEM((2, 8, 80, 256), F32),
             pltpu.VMEM((2, 8, 80, 256), F32),
             pltpu.VMEM((2, 8, 2, 80, 256), F32),
             pltpu.VMEM((own_width, 256, 512), BF16),
+            pltpu.VMEM((32, own_width * low, 128), BF16),
+            pltpu.VMEM((4, 176, 128), F32),
+            pltpu.VMEM(targets.shape, F32),
             pltpu.VMEM((2, 256, 128), F32),
             pltpu.VMEM((2, 256, 128), F32),
             pltpu.VMEM((4, 2, 64, 128), F32),
             pltpu.VMEM((width, 512), BF16),
             pltpu.VMEM((256, 512), BF16),
             dma((16,)),
-            dma((chunks + 1,)),
-            dma((chunks + 1,)),
+            dma,
+            dma((2 * chunks,)),
+            dma((2 * chunks,)),
             dma((chunks + 1,)),
             dma((chunks + 1,)),
             dma((chunks + 1,)),

time: 261 us -> 233 us (0.89)
  Pallas kernels: 255 us -> 228 us
    pallas_call x1, Pallas kernels: 255 us -> 228 us  [on_device(): pl.pallas_call(kernel, out_shape=(jax.ShapeDtypeStruct(targets.shape, F32...]
where the time goes in v3:
time: 233 us
  Pallas kernels  228 us (98%)
  local copies, waits for them, and re-layouts  3.61 us (2%)
    pallas_call x1, Pallas kernels, on_device(): pl.pallas_call(kernel, out_shape=(jax.ShapeDtypeStruct(targets.shape, F32...  228 us

profile of v3, /device:TPU:1, one launch (start us, length us, event | category | flops | bytes accessed | tf_op | source)
XLA Modules:
  0.0 232.7 jit_solution(15881454001499562952)
XLA Ops:
  0.6 228.5 %shard_map.139 = (f32[73,30,120]{2,1,0:T(8,128)}, f32[1,48,60]{2,1,0:T(8,128)}, f32[1,48,60]{2,1,0:T(8,128)}) custom-call(bf16[1,30,120,384]{3,2,1,0:T(8,128)(2,1)} %fields_hbm.1, f32[73,30,120]{2,1,0:T(8,128)} %targets_hbm.1, f32[1,48,60]{2,1,0:T(8,128)} %bitcast.6, f32[1,48,60]{2,1,0:T(8,128)} %bitcast.7, bf16[1,384,384]{2,1,0:T(8,128)(2,1)} %w_hbm.1, ...), custom_call_target="tpu_custom_call" | custom-call | tf_op jit(solution)/shard_map/pallas_call | solution.py:523
  229.1 0.0 copy-start.1
  229.1 0.0 copy-start
  229.1 2.4 %copy.18 = f32[73,30,120]{2,1,0:T(8,128)} copy(f32[73,30,120]{2,1,0:T(8,128)} %get-tuple-element.12) | data formatting | bytes 2102400
  231.5 0.0 copy-done.1
  231.5 0.6 copy.19
  232.1 0.0 copy-done
  232.1 0.6 copy.20
Async XLA Ops:
  229.1 2.4 %copy-start.1 = (f32[1,48,60]{2,1,0:T(8,128)S(1)}, f32[1,48,60]{2,1,0:T(8,128)}, u32[]{:S(2)}) copy-start(f32[1,48,60]{2,1,0:T(8,128)} %get-tuple-element.7) | copy-start | bytes 34564
  229.1 3.0 %copy-start = (f32[1,48,60]{2,1,0:T(8,128)S(1)}, f32[1,48,60]{2,1,0:T(8,128)}, u32[]{:S(2)}) copy-start(f32[1,48,60]{2,1,0:T(8,128)} %get-tuple-element.8) | copy-start | bytes 34564

commit v4 on v3

--- a/solution.py
+++ b/solution.py
@@ -47,6 +47,10 @@
     return jnp.dot(a, b, preferred_element_type=F32)
 
 
+def logistic(v):
+    return 0.5 * jnp.tanh(0.5 * v) + 0.5
+
+
 def wait_for(ref, sem):
     pltpu.make_async_copy(ref, ref, sem).wait()
 
@@ -59,7 +63,7 @@
     goal, loss_rows, filters, square, w_t, b_col, wo_pad, wo_t, bo_col,
     cells, fields_t, block, block_low, grid, grid_low, spatial, spatial_low, back, back_low,
     spectrum, preact, pred, pred_in, sums, ggrid, ggrid_low, line, nll_all,
-    weights, gsum, gsum_in, mixed, gpair,
+    filters_in, weights, gsum, gsum_in, mixed, gpair,
     load_sem, nll_sem, out_sem, in_sem, back_out, back_in, gout_sem, gin_sem, pred_out, pred_in_sem,
     sums_out, sums_in, fwd_out, fwd_in, filt_out, filt_in, grad_out, grad_in,
 ):
@@ -199,25 +203,27 @@
 
     for copy in later[:2]:
         copy.wait()
-    for n, part in enumerate((fre, fim)):
-        square[...] = jnp.zeros_like(square)
-        square[0:48, 0:60] = part[0]
-        filters[n] = square[...].T[0:64]
+    filters[...] = jnp.zeros_like(filters)
+    for lo in range(4):
+        mine = slice(lo * own_width, (lo + 1) * own_width)
+        filters[lo, 0:own_width, 0:60] = fre[0, mine, :]
+        filters[lo, own_width : 2 * own_width, 0:60] = fim[0, mine, :]
 
     pl.semaphore_wait(barrier, 31 + 7)
 
     @pl.loop(1, 4)
     def _(o):
+        lo = (ilon + o) % 4
         pltpu.make_async_remote_copy(
-            filters,
-            weights.at[:, pl.ds(pl.multiple_of(ilon * 64, 64), 64), :],
+            filters.at[lo],
+            filters_in.at[ilon],
             filt_out,
             filt_in,
-            device_id=(im, ilat, (ilon + o) % 4),
+            device_id=(im, ilat, lo),
             device_id_type=MESH_ID,
         ).start()
 
-    weights[:, pl.ds(pl.multiple_of(ilon * 64, 64), 64), :] = filters[...]
+    filters_in[ilon] = filters[ilon]
 
     to_owners(grid, 0, chunk, out_sem.at[0], in_sem.at[0])
 
@@ -263,7 +269,11 @@
 
     gpair[...] = jnp.zeros_like(gpair)
     gsum[...] = jnp.zeros_like(gsum)
-    wait_for(weights.at[:, pl.ds(0, 192), :], filt_in)
+    wait_for(filters_in.at[pl.ds(0, 3)], filt_in)
+    square[...] = jnp.zeros_like(square)
+    for lo in range(4):
+        square[0 : 2 * own_width] = filters_in[lo]
+        weights[lo * 64 : (lo + 1) * 64] = square[...].T[0:64]
 
     lane = lax.broadcasted_iota(jnp.int32, (256, 128), 1)
     k_row = lax.broadcasted_iota(jnp.int32, (256, 256), 0)
@@ -279,9 +289,9 @@
 
         @pl.loop(ch * chunk, (ch + 1) * chunk)
         def _(c):
-            own = lane == ilon * own_width + c
-            wr = jnp.sum(jnp.where(own, weights[0], 0.0), axis=1, keepdims=True)
-            wi = jnp.sum(jnp.where(own, weights[1], 0.0), axis=1, keepdims=True)
+            both = weights[...]
+            wr = jnp.sum(jnp.where(lane == c, both, 0.0), axis=1, keepdims=True)
+            wi = jnp.sum(jnp.where(lane == own_width + c, both, 0.0), axis=1, keepdims=True)
             spectrum[c] = to_spectral(grid[c])
             sr, si = spectrum[c, :, 0:256], spectrum[c, :, 256:512]
             fr = jnp.where(keep, wr * sr - wi * si, 0.0).astype(BF16)
@@ -335,7 +345,7 @@
         bias = b_col[...]
         pa = mm(w_t[...], mixed[...]) + jnp.concatenate([bias] * 4, axis=1)
         preact[u] = pa
-        hidden = (pa / (1.0 + jnp.exp(-pa))).astype(BF16)
+        hidden = (pa * logistic(pa)).astype(BF16)
         bias = bo_col[0:80, :]
         out = mm(wo_pad[0:80, :].astype(BF16), hidden) + jnp.concatenate([bias] * 4, axis=1)
         pred[half, 2 * i] = out[:, 0:256]
@@ -412,7 +422,7 @@
         gpair[128:208, :] = (gp - high.astype(F32)).astype(BF16)
         gh = mm(wo_t[...], gpair[...])
         pa = preact[u]
-        sg = 1.0 / (1.0 + jnp.exp(-pa))
+        sg = logistic(pa)
         gpre = (gh * sg * (1.0 + pa * (1.0 - sg))).astype(BF16)
         gm = mm(w[0], gpre)
         for q in range(4):
@@ -465,20 +475,24 @@
 
         @pl.loop(ch * chunk, (ch + 1) * chunk)
         def _(c):
-            own = lane == ilon * own_width + c
             g = to_spectral(ggrid[c])
             gr, gi = g[:, 0:256], g[:, 256:512]
             sr, si = spectrum[c, :, 0:256], spectrum[c, :, 256:512]
             g_re = jnp.sum(jnp.where(keep, gr * sr + gi * si, 0.0), axis=1, keepdims=True)
             g_im = jnp.sum(jnp.where(keep, gi * sr - gr * si, 0.0), axis=1, keepdims=True)
-            gsum[0] = gsum[0] + jnp.where(own, g_re, 0.0)
-            gsum[1] = gsum[1] + jnp.where(own, g_im, 0.0)
+            both = jnp.where(lane == c, g_re, gsum[...])
+            gsum[...] = jnp.where(lane == own_width + c, g_im, both)
+
+    wait_for(filters.at[pl.ds(0, 3)], filt_out)
+    for lo in range(4):
+        square[0:64] = gsum[lo * 64 : (lo + 1) * 64]
+        filters[lo] = square[...].T[0 : 2 * own_width]
 
     @pl.loop(1, 4)
     def _(o):
         lo = (ilon + o) % 4
         pltpu.make_async_remote_copy(
-            gsum.at[:, pl.ds(pl.multiple_of(lo * 64, 64), 64), :],
+            filters.at[lo],
             gsum_in.at[ilon],
             grad_out,
             grad_in,
@@ -486,12 +500,12 @@
             device_id_type=MESH_ID,
         ).start()
 
-    gsum_in[ilon] = gsum[:, pl.ds(pl.multiple_of(ilon * 64, 64), 64), :]
+    gsum_in[ilon] = filters[ilon]
     wait_for(gsum_in.at[pl.ds(0, 3)], grad_in)
-    total = gsum_in[0] + gsum_in[1] + gsum_in[2] + gsum_in[3]
-    for n, part in enumerate((grad_re, grad_im)):
-        square[0:64] = total[n]
-        part[0] = square[...].T[0:48, 0:60]
+    for lo in range(4):
+        mine = slice(lo * own_width, (lo + 1) * own_width)
+        grad_re[0, mine, :] = gsum_in[lo, 0:own_width, 0:60]
+        grad_im[0, mine, :] = gsum_in[lo, own_width : 2 * own_width, 0:60]
 
     for ch in range(chunks):
         wait_31(chunk, back_out.at[ch])
@@ -506,7 +520,6 @@
             wait_for(sums.at[half, 0], sums_out.at[half, t])
         for t in (1, 2, 3):
             wait_for(sums.at[half, 0], fwd_out.at[half, t])
-    wait_for(weights.at[:, pl.ds(0, 192), :], filt_out)
     wait_for(gsum_in.at[pl.ds(0, 3)], grad_out)
 
 
@@ -544,7 +557,7 @@
             pltpu.VMEM((512, 512), BF16),
             pltpu.VMEM((80 * 32, 128), F32),
             pltpu.VMEM((80 * 32, 128), F32),
-            pltpu.VMEM((2, 64, 128), F32),
+            pltpu.VMEM((4, 2 * own_width, 128), F32),
             pltpu.VMEM((128, 128), F32),
             pltpu.VMEM((width, width), BF16),
             pltpu.VMEM((width, 128), F32),
@@ -570,9 +583,10 @@
             pltpu.VMEM((32, own_width * low, 128), BF16),
             pltpu.VMEM((4, 176, 128), F32),
             pltpu.VMEM(targets.shape, F32),
-            pltpu.VMEM((2, 256, 128), F32),
-            pltpu.VMEM((2, 256, 128), F32),
-            pltpu.VMEM((4, 2, 64, 128), F32),
+            pltpu.VMEM((4, 2 * own_width, 128), F32),
+            pltpu.VMEM((256, 128), F32),
+            pltpu.VMEM((256, 128), F32),
+            pltpu.VMEM((4, 2 * own_width, 128), F32),
             pltpu.VMEM((width, 512), BF16),
             pltpu.VMEM((256, 512), BF16),
             dma((16,)),

time: 233 us -> 222 us (0.953)
  Pallas kernels: 228 us -> 218 us
    pallas_call x1, Pallas kernels: 228 us -> 218 us  [on_device(): pl.pallas_call(kernel, out_shape=(jax.ShapeDtypeStruct(targets.shape, F32...]
where the time goes in v4:
time: 222 us
  Pallas kernels  218 us (98%)
  local copies, waits for them, and re-layouts  3.61 us (2%)
    pallas_call x1, Pallas kernels, on_device(): pl.pallas_call(kernel, out_shape=(jax.ShapeDtypeStruct(targets.shape, F32...  218 us

profile of v4, /device:TPU:1, one launch (start us, length us, event | category | flops | bytes accessed | tf_op | source)
XLA Modules:
  0.0 222.3 jit_solution(3655964319020517138)
XLA Ops:
  0.6 218.1 %shard_map.139 = (f32[73,30,120]{2,1,0:T(8,128)}, f32[1,48,60]{2,1,0:T(8,128)}, f32[1,48,60]{2,1,0:T(8,128)}) custom-call(bf16[1,30,120,384]{3,2,1,0:T(8,128)(2,1)} %fields_hbm.1, f32[73,30,120]{2,1,0:T(8,128)} %targets_hbm.1, f32[1,48,60]{2,1,0:T(8,128)} %bitcast.6, f32[1,48,60]{2,1,0:T(8,128)} %bitcast.7, bf16[1,384,384]{2,1,0:T(8,128)(2,1)} %w_hbm.1, ...), custom_call_target="tpu_custom_call" | custom-call | tf_op jit(solution)/shard_map/pallas_call | solution.py:536
  218.7 0.0 copy-start.1
  218.7 0.0 copy-start
  218.7 2.4 %copy.18 = f32[73,30,120]{2,1,0:T(8,128)} copy(f32[73,30,120]{2,1,0:T(8,128)} %get-tuple-element.12) | data formatting | bytes 2102400
  221.1 0.0 copy-done.1
  221.1 0.6 copy.19
  221.7 0.0 copy-done
  221.7 0.6 copy.20
Async XLA Ops:
  218.7 2.4 %copy-start.1 = (f32[1,48,60]{2,1,0:T(8,128)S(1)}, f32[1,48,60]{2,1,0:T(8,128)}, u32[]{:S(2)}) copy-start(f32[1,48,60]{2,1,0:T(8,128)} %get-tuple-element.7) | copy-start | bytes 34564
  218.7 3.0 %copy-start = (f32[1,48,60]{2,1,0:T(8,128)S(1)}, f32[1,48,60]{2,1,0:T(8,128)}, u32[]{:S(2)}) copy-start(f32[1,48,60]{2,1,0:T(8,128)} %get-tuple-element.8) | copy-start | bytes 34564

commit v5 on v4

--- a/solution.py
+++ b/solution.py
@@ -15,6 +15,8 @@
 rows, columns, width, variables, members = 240, 480, 384, 73, 8
 own_rows, own_columns, own_width = 30, 120, 12
 low = 14
+low_rows = own_width * low
+sent_rows = low_rows - 8
 chunks = 3
 chunk = own_width // chunks
 variance_floor = 0.1
@@ -62,10 +64,10 @@
     fields, targets, fre, fim, w, b, wo, bo, lat, lat_t, lon, lon_t,
     goal, loss_rows, filters, square, w_t, b_col, wo_pad, wo_t, bo_col,
     cells, fields_t, block, block_low, grid, grid_low, spatial, spatial_low, back, back_low,
-    spectrum, preact, pred, pred_in, sums, ggrid, ggrid_low, line, nll_all,
+    spectrum, preact, pred, pred_in, sums, ggrid, ggrid_low, line, tail, nll_all,
     filters_in, weights, gsum, gsum_in, mixed, gpair,
     load_sem, nll_sem, out_sem, in_sem, back_out, back_in, gout_sem, gin_sem, pred_out, pred_in_sem,
-    sums_out, sums_in, fwd_out, fwd_in, filt_out, filt_in, grad_out, grad_in,
+    back_low_in, gin_low, sums_out, sums_in, fwd_out, fwd_in, filt_out, filt_in, grad_out, grad_in,
 ):
     im = lax.axis_index("member")
     ilat = lax.axis_index("lat")
@@ -73,11 +75,17 @@
     me = ilat * 4 + ilon
     partner = (im // 2) * 2 + 1 - im % 2
 
-    def peer(o):
+    def peer(o, sign=1):
+        o = (32 - o) % 32
         y, z = ilat % 4, (ilat // 4) * 4 + ilon
-        y2, z2 = (y + o % 4) % 4, (z + o // 4) % 8
+        turn_z = sign * ((o % 8 + 1) // 2) * (2 * (o % 2) - 1)
+        y2, z2 = (y + sign * (o // 8) + 4) % 4, (z + turn_z + 8) % 8
         la, lo = (z2 // 4) * 4 + y2, z2 % 4
         return (im, la, lo), la, lo
+
+    def source(o):
+        _, la, lo = peer(o, -1)
+        return la, lo
 
     def at_member(m):
         return (m, ilat, ilon)
@@ -124,7 +132,7 @@
         return (pl.ds((la * 4 + lo) * own_width + c0, n),)
 
     def low_part(c0, n, la, lo):
-        return (la * 4 + lo, pl.ds(c0 * low, n * low))
+        return (la * 4 + lo, pl.ds(c0 * low, min((c0 + n) * low, sent_rows) - c0 * low))
 
     def exchange(src, src_part, dst, dst_part, c0, n, sem_out, sem_in):
         @pl.loop(1, 32)
@@ -150,8 +158,8 @@
     def wait_31(n, sem):
         wait_for(block.at[pl.ds(0, 31 * n)], sem)
 
-    def wait_low(n, sem):
-        wait_for(block_low.at[pl.ds(0, 31), pl.ds(0, n * low)], sem)
+    def wait_low(c0, n, sem):
+        wait_for(block_low.at[(pl.ds(0, 31), *low_part(c0, n, 0, 0)[1:])], sem)
 
     def turn(j, q):
         x = fields[j].astype(F32)
@@ -165,6 +173,24 @@
             for c in range(8):
                 part = cells[pl.ds(pl.multiple_of(i * 256 + c * 32, 32), 16), :]
                 block[i * 8 + c] = part.astype(BF16)
+
+    lane8 = lax.broadcasted_iota(jnp.int32, (8, 128), 1)
+
+    def fold(rows_of):
+        last = rows_of[sent_rows:low_rows, :]
+        for i in range(15):
+            moved = pltpu.roll(last, (120 - 8 * i) % 128, 1)
+            rows_of[8 * i : 8 * i + 8, :] = jnp.where(
+                lane8 >= own_columns, moved, rows_of[8 * i : 8 * i + 8, :]
+            )
+
+    def unfold(rows_of, first, end):
+        last = jnp.zeros((8, 128), F32)
+        for i in range(first // 8, end // 8):
+            part = rows_of[8 * i : 8 * i + 8, :].astype(F32)
+            moved = pltpu.roll(part, (8 * i - 120) % 128, 1)
+            last = jnp.where(lane8 // 8 == i, moved, last)
+        return last
 
     def fill_low():
         @pl.loop(0, 16)
@@ -174,20 +200,35 @@
                 for c in range(own_width):
                     first = pl.multiple_of((d * own_width + c) * 32 + 16, 16)
                     line[e, pl.ds(c * low, 16), :] = cells[pl.ds(first, 16), :]
-                block_low[d] = line[e, 0 : own_width * low, :].astype(BF16)
-
-    def spread_low(src, target, ch):
+                fold(line.at[e])
+                block_low[d] = line[e, 0:sent_rows, :].astype(BF16)
+
+    def spread_low(src, target, ch, sems=None):
+        first = ch * chunk * low
+        sent = min(first + chunk * low, sent_rows) - first
+
         @pl.loop(0, 8)
-        def _(la):
-            for lo in range(4):
-                part = src[la * 4 + lo, pl.ds(ch * chunk * low, chunk * low)]
-                line[lo, 0 : chunk * low, :] = part.astype(F32)
+        def _(i):
+            for e in range(4):
+                la, lo = source(i * 4 + e)
+                s = la * 4 + lo
+                if sems is not None:
+
+                    @pl.when(i * 4 + e > 0)
+                    def _():
+                        wait_for(src.at[s, pl.ds(first, sent)], sems.at[s])
+
+                line[e, 0:sent, :] = src[s, pl.ds(first, sent)].astype(F32)
+                if ch == chunks - 2:
+                    tail[s] = unfold(src.at[s], 0, first + sent)
+                if ch == chunks - 1:
+                    line[e, sent : sent + 8, :] = tail[s] + unfold(src.at[s], first, 120)
                 for c in range(chunk):
                     target[
                         ch * chunk + c,
                         pl.ds(pl.multiple_of(128 + la * 16, 16), 16),
-                        lo * 128 : (lo + 1) * 128,
-                    ] = line[lo, pl.ds(c * low, 16), :].astype(BF16)
+                        pl.ds(pl.multiple_of(lo * 128, 128), 128),
+                    ] = line[e, pl.ds(c * low, 16), :].astype(BF16)
 
     line[...] = jnp.zeros_like(line)
 
@@ -284,7 +325,7 @@
 
     for ch in range(chunks):
         wait_31(chunk, in_sem.at[ch])
-        wait_low(chunk, in_sem.at[chunks + ch])
+        wait_low(ch * chunk, chunk, in_sem.at[chunks + ch])
         spread_low(grid_low, grid, ch)
 
         @pl.loop(ch * chunk, (ch + 1) * chunk)
@@ -309,14 +350,17 @@
             spatial, grid_part, back, block_part, ch * chunk, chunk, back_out.at[ch], back_in.at[ch]
         )
 
-    @pl.loop(0, 32)
-    def _(d):
-        part = cells[pl.ds(pl.multiple_of(d * 176, 16), own_width * low), :]
-        spatial_low[d] = part.astype(BF16)
+    @pl.loop(0, 16)
+    def _(i):
+        for e in range(2):
+            d = i * 2 + e
+            line[e, 0:low_rows, :] = cells[pl.ds(pl.multiple_of(d * 176, 16), low_rows), :]
+            fold(line.at[e])
+            spatial_low[d] = line[e, 0:sent_rows, :].astype(BF16)
 
     exchange(
         spatial_low, low_part, back_low, low_part, 0, own_width,
-        back_out.at[chunks], back_in.at[chunks],
+        back_out.at[chunks], back_low_in.at[me],
     )
 
     def unpack(ch):
@@ -330,8 +374,15 @@
         @pl.loop(0, 16)
         def _(i):
             for e in range(2):
-                s = i * 2 + e
-                line[e, 0 : own_width * low, :] = back_low[s].astype(F32)
+                la, lo = source(i * 2 + e)
+                s = la * 4 + lo
+
+                @pl.when(i * 2 + e > 0)
+                def _():
+                    wait_for(back_low.at[s], back_low_in.at[s])
+
+                line[e, 0:sent_rows, :] = back_low[s].astype(F32)
+                line[e, sent_rows:low_rows, :] = unfold(back_low.at[s], 0, 120)
                 for c in range(own_width):
                     first = pl.multiple_of((s * own_width + c) * 32 + 16, 16)
                     cells[pl.ds(first, 16), :] = line[e, pl.ds(c * low, 16), :]
@@ -391,11 +442,11 @@
             second = second + one * one
         sums[half, im, 0] = first
         sums[half, im, 1] = second
-        for t in (1, 2, 3):
+        sums_copy(half, im, partner, sums_out.at[half, 0], sums_in.at[half, 0]).start()
+        for t in (1, 3, 2):
             sums_copy(
                 half, im, (im + 2 * t) % 8, sums_out.at[half, t], sums_in.at[half, t]
             ).start()
-        sums_copy(half, im, partner, sums_out.at[half, 0], sums_in.at[half, 0]).start()
 
     def backward(half, i):
         u = half * 4 + i
@@ -429,17 +480,33 @@
             cells[pl.ds(4 * u + q, width, stride=32), :] = gm[:, q * 128 : (q + 1) * 128]
 
     def backward_half(half):
-        wait_for(sums.at[half, 0], sums_in.at[half, 0])
-        backward(half, im // 2)
-        for t in (1, 2, 3):
+        def pass_on(t):
             wait_for(sums.at[half, 0], sums_in.at[half, t])
             sums_copy(
                 half, (im + 8 - 2 * t) % 8, partner, fwd_out.at[half, t], fwd_in.at[half, t]
             ).start()
 
-        @pl.loop(1, 4)
-        def _(t):
-            wait_for(sums.at[half, 0], fwd_in.at[half, t])
+        @pl.loop(0, 4)
+        def _(i):
+            t = i + (i // 2) * (1 - 2 * (i % 2))
+
+            @pl.when(i == 0)
+            def _():
+                wait_for(sums.at[half, 0], sums_in.at[half, 0])
+
+            @pl.when(i == 1)
+            def _():
+                pass_on(1)
+                pass_on(3)
+
+            @pl.when(i == 2)
+            def _():
+                pass_on(2)
+
+            @pl.when(i > 0)
+            def _():
+                wait_for(sums.at[half, 0], fwd_in.at[half, t])
+
             backward(half, (im // 2 + 4 - t) % 4)
 
     for ch in range(chunks):
@@ -448,19 +515,19 @@
     decode_half(0)
     for ch in range(chunks):
         wait_31(chunk, out_sem.at[ch])
-        wait_low(chunk, out_sem.at[chunks + ch])
+        wait_low(ch * chunk, chunk, out_sem.at[chunks + ch])
     sum_half(0)
     backward_half(0)
     fill_block()
     to_owners(ggrid, 0, own_width, gout_sem.at[chunks], gin_sem.at[chunks])
-    wait_low(own_width, back_in.at[chunks])
     unpack_low()
     decode_half(1)
     sum_half(1)
     backward_half(1)
     fill_low()
     for ch in range(chunks):
-        low_to_owners(ggrid_low, ch * chunk, chunk, gout_sem.at[ch], gin_sem.at[ch])
+        arrival = gin_sem.at[ch] if ch < chunks - 1 else gin_low.at[me]
+        low_to_owners(ggrid_low, ch * chunk, chunk, gout_sem.at[ch], arrival)
 
     @pl.loop(0, variables)
     def _(v):
@@ -470,8 +537,11 @@
     nll_copy.start()
     wait_31(own_width, gin_sem.at[chunks])
     for ch in range(chunks):
-        wait_low(chunk, gin_sem.at[ch])
-        spread_low(ggrid_low, ggrid, ch)
+        if ch < chunks - 1:
+            wait_low(ch * chunk, chunk, gin_sem.at[ch])
+            spread_low(ggrid_low, ggrid, ch)
+        else:
+            spread_low(ggrid_low, ggrid, ch, gin_low)
 
         @pl.loop(ch * chunk, (ch + 1) * chunk)
         def _(c):
@@ -509,10 +579,10 @@
 
     for ch in range(chunks):
         wait_31(chunk, back_out.at[ch])
-    wait_low(own_width, back_out.at[chunks])
+    wait_low(0, own_width, back_out.at[chunks])
     wait_31(own_width, gout_sem.at[chunks])
     for ch in range(chunks):
-        wait_low(chunk, gout_sem.at[ch])
+        wait_low(ch * chunk, chunk, gout_sem.at[ch])
     nll_copy.wait()
     for half in range(2):
         wait_for(pred.at[half, pl.ds(0, 7)], pred_out.at[half])
@@ -521,6 +591,26 @@
         for t in (1, 2, 3):
             wait_for(sums.at[half, 0], fwd_out.at[half, t])
     wait_for(gsum_in.at[pl.ds(0, 3)], grad_out)
+
+
+def finish(nll_in, re_in, im_in, nll, grad_re, grad_im, nll_all, re, im, in_sem, out_sem):
+    pieces = [(nll_in, nll_all, nll, pl.ds(i * 19, min(19, variables - i * 19))) for i in range(4)]
+    pieces += [(re_in, re, grad_re, pl.ds(0, 1)), (im_in, im, grad_im, pl.ds(0, 1))]
+    reads = [
+        pltpu.make_async_copy(src.at[at], mid.at[at], in_sem.at[i])
+        for i, (src, mid, _, at) in enumerate(pieces)
+    ]
+    writes = [
+        pltpu.make_async_copy(mid.at[at], dst.at[at], out_sem.at[i])
+        for i, (_, mid, dst, at) in enumerate(pieces)
+    ]
+    for read in reads:
+        read.start()
+    for read, write in zip(reads, writes):
+        read.wait()
+        write.start()
+    for write in writes:
+        write.wait()
 
 
 def on_device(fields, targets, filt_re, filt_im, w_in, b_in, w_out, b_out):
@@ -567,21 +657,22 @@
             pltpu.VMEM((width * 32, 128), F32),
             pltpu.VMEM((8, width, 512), BF16),
             pltpu.VMEM((width, 16, 128), BF16),
-            pltpu.VMEM((32, own_width * low, 128), BF16),
+            pltpu.VMEM((32, sent_rows, 128), BF16),
             pltpu.VMEM((own_width, 256, 512), BF16),
-            pltpu.VMEM((32, own_width * low, 128), BF16),
+            pltpu.VMEM((32, sent_rows, 128), BF16),
             pltpu.VMEM((own_width, 128, 512), BF16),
-            pltpu.VMEM((32, own_width * low, 128), BF16),
+            pltpu.VMEM((32, sent_rows, 128), BF16),
             pltpu.VMEM((width, 16, 128), BF16),
-            pltpu.VMEM((32, own_width * low, 128), BF16),
+            pltpu.VMEM((32, sent_rows, 128), BF16),
             pltpu.VMEM((own_width, 256, 512), F32),
             pltpu.VMEM((8, width, 512), F32),
             pltpu.VMEM((2, 8, 80, 256), F32),
             pltpu.VMEM((2, 8, 80, 256), F32),
             pltpu.VMEM((2, 8, 2, 80, 256), F32),
             pltpu.VMEM((own_width, 256, 512), BF16),
-            pltpu.VMEM((32, own_width * low, 128), BF16),
+            pltpu.VMEM((32, sent_rows, 128), BF16),
             pltpu.VMEM((4, 176, 128), F32),
+            pltpu.VMEM((32, 8, 128), F32),
             pltpu.VMEM(targets.shape, F32),
             pltpu.VMEM((4, 2 * own_width, 128), F32),
             pltpu.VMEM((256, 128), F32),
@@ -599,6 +690,8 @@
             dma((chunks + 1,)),
             dma((2,)),
             dma((2,)),
+            dma((32,)),
+            dma((32,)),
             dma((2, 4)),
             dma((2, 4)),
             dma((2, 4)),
@@ -612,6 +705,14 @@
             collective_id=0, has_side_effects=True, vmem_limit_bytes=67043328
         ),
     )(fields, targets, filt_re, filt_im, w_in, b_in, w_out, b_out, lat, lat_t, lon, lon_t)
+    shapes = (nll.shape, grad_re.shape, grad_im.shape)
+    nll, grad_re, grad_im = pl.pallas_call(
+        finish,
+        out_shape=tuple(jax.ShapeDtypeStruct(shape, F32) for shape in shapes),
+        in_specs=[anywhere] * 3,
+        out_specs=(anywhere,) * 3,
+        scratch_shapes=[pltpu.VMEM(shape, F32) for shape in shapes] + [dma((6,)), dma((6,))],
+    )(nll, grad_re, grad_im)
     return nll, jnp.swapaxes(grad_re, 1, 2), jnp.swapaxes(grad_im, 1, 2)
 
 

time: 222 us -> 212 us (0.955)
  Pallas kernels: 218 us -> 210 us
  local copies, waits for them, and re-layouts: 3.61 us -> 0 us
    pallas_call x1, Pallas kernels: 218 us -> 208 us  [on_device(): pl.pallas_call(kernel, out_shape=(jax.ShapeDtypeStruct(targets.shape, F32...]
    unnamed x7 -> x0, local copies, waits for them, and re-layouts: 3.61 us -> none
where the time goes in v5:
time: 212 us; the launch traced here: 211 us
  Pallas kernels  210 us (99%)
    pallas_call x1, Pallas kernels, on_device(): pl.pallas_call(kernel, out_shape=(jax.ShapeDtypeStruct(targets.shape, F32...  208 us

profile of v5, /device:TPU:1, one launch (start us, length us, event | category | flops | bytes accessed | tf_op | source)
XLA Modules:
  0.0 210.9 jit_solution(292891212543826365)
XLA Ops:
  0.6 208.2 %shard_map.139 = (f32[73,30,120]{2,1,0:T(8,128)}, f32[1,48,60]{2,1,0:T(8,128)}, f32[1,48,60]{2,1,0:T(8,128)}) custom-call(bf16[1,30,120,384]{3,2,1,0:T(8,128)(2,1)} %fields_hbm.1, f32[73,30,120]{2,1,0:T(8,128)} %targets_hbm.1, f32[1,48,60]{2,1,0:T(8,128)} %bitcast.4, f32[1,48,60]{2,1,0:T(8,128)} %bitcast.5, bf16[1,384,384]{2,1,0:T(8,128)(2,1)} %w_hbm.1, ...), custom_call_target="tpu_custom_call" | custom-call | tf_op jit(solution)/shard_map/pallas_call | solution.py:626
  208.8 2.1 shard_map.140
